TPU v7x, 1024 devices: a whole 8x8x8 slice. The times are simulated.
1024 devices in a mesh: expert: 64 (over y, x), dp: 16 (over z, core).
Axes of the slice: x: 8, y: 8, z: 8, core: 2. Of those that a mesh axis runs over, the one named last changes fastest.
Arguments:
- tokens: bfloat16 [16384, 2048], P(('dp', 'expert')), may hold values from -6 to 6
- cotangent: bfloat16 [16384, 8, 384], P(('dp', 'expert')), may hold values from -1 to 1
- expert_ids: int32 [16384, 8], P(('dp', 'expert')), may hold values from 0 to 31, all different within a row; in each aligned block of 16 rows (0 to 15, 16 to 31, ...) at most 5 rows name the same one
- placement: int32 [64], replicated, may hold values from 0 to 31, as said below
- master: float32 [32, 1572864], P(None, ('dp', 'expert')), may hold values from -0.125 to 0.125
- first_moment: float32 [32, 1572864], P(None, ('dp', 'expert')), may hold values from -12 to 12
- second_moment: float32 [32, 1572864], P(None, ('dp', 'expert')), may hold values from 1 to 30
Outputs:
- new_master: float32 [32, 1572864], P(None, ('dp', 'expert'))
- new_first: float32 [32, 1572864], P(None, ('dp', 'expert'))
- new_second: float32 [32, 1572864], P(None, ('dp', 'expert'))
- replica_grad: float32 [64, 384, 4096], P('expert', 'dp')
Inputs may be any that keep to these rules, and one draw needn't show every extreme that they name: `expert_ids`: among the tokens of one device no expert is named more than 5 times; some device names some expert exactly 5 times. `placement`: every one of the 32 experts holds at least one of the 64 slots.
All inputs are finite; a program needn't handle non-finite values.
Results may differ from a plain program's by a relative error of at most 0.017.
Values may be sent and summed in bfloat16 or wider, within the bound.
No kernel may reach another device: no remote copies, remote signals or barrier semaphores. Data moves between devices by JAX's collectives and lax.ppermute only.
A program may use at most 64 MiB of HBM per device.

v0:
```python
import jax
import jax.numpy as jnp
from jax import lax
from jax.sharding import PartitionSpec as P

MOST = 5


beta_first = 0.9
beta_second = 0.95
learning_rate = 0.01
decay_rate = 0.1
epsilon = 1e-08
adam_steps = 20.0


def adamw_update(master, first_moment, second_moment, grads):
    new_first = beta_first * first_moment + (1.0 - beta_first) * grads
    new_second = beta_second * second_moment + (1.0 - beta_second) * grads * grads
    corr_first = 1.0 - beta_first**adam_steps
    corr_second = 1.0 - beta_second**adam_steps
    update = (
        new_first / corr_first / (jnp.sqrt(new_second / corr_second) + epsilon)
        + decay_rate * master
    )
    return (master - learning_rate * update, new_first, new_second)


def local(tokens, cotangent, expert_ids, placement, master, first_moment, second_moment):
    expert_devices = lax.axis_size("expert")
    source_index = lax.axis_index("expert")
    slot_count = placement.shape[0]
    slot_local = slot_count // expert_devices
    expert_count = master.shape[0]
    shard_width = master.shape[1]
    token_rows = tokens.shape[0]
    model_width = tokens.shape[1]
    top_count = expert_ids.shape[1]
    hidden_width = cotangent.shape[2]
    assigned = token_rows * top_count
    piece_rows = shard_width * expert_devices // (2 * model_width)
    send_total = slot_count * MOST
    expert_range = jnp.arange(expert_count, dtype=jnp.int32)
    slot_range = jnp.arange(slot_count, dtype=jnp.int32)
    slot_hot = placement[:, None] == expert_range[None, :]
    replicas = jnp.sum(slot_hot.astype(jnp.int32), axis=0)
    earlier_same = (slot_range[:, None] > slot_range[None, :]) & (
        placement[:, None] == placement[None, :]
    )
    slot_rank = jnp.sum(earlier_same.astype(jnp.int32), axis=1)
    wanted = jnp.mod(source_index, replicas)
    target_hot = slot_hot & (slot_rank[:, None] == wanted[None, :])
    target_slot = jnp.sum(jnp.where(target_hot, slot_range[:, None], 0), axis=0)
    flat_ids = expert_ids.reshape(assigned)
    expert_hot = flat_ids[:, None] == expert_range[None, :]
    earlier = jnp.cumsum(expert_hot.astype(jnp.int32), axis=0) - 1
    position = jnp.sum(jnp.where(expert_hot, earlier, 0), axis=1)
    destination = jnp.sum(jnp.where(expert_hot, target_slot[None, :], 0), axis=1)
    target_device = destination // slot_local
    local_slot = destination % slot_local
    send_row = (local_slot * expert_devices + target_device) * MOST + position
    copy_range = jnp.arange(assigned, dtype=jnp.int32)
    row_match = jnp.arange(send_total, dtype=jnp.int32)[:, None] == send_row[None, :]
    filled = jnp.any(row_match, axis=1)
    source_copy = jnp.sum(jnp.where(row_match, copy_range[None, :], 0), axis=1)
    gathered_x = jnp.take(tokens, source_copy // top_count, axis=0)
    send_x = jnp.where(filled[:, None], gathered_x, jnp.zeros_like(gathered_x))
    send_x = send_x.reshape(slot_local, expert_devices, MOST, model_width)
    gathered_dh = jnp.take(cotangent.reshape(assigned, hidden_width), source_copy, axis=0)
    send_dh = jnp.where(filled[:, None], gathered_dh, jnp.zeros_like(gathered_dh))
    send_dh = send_dh.reshape(slot_local, expert_devices, MOST, hidden_width)
    piece_expert = placement.reshape(expert_devices, slot_local).T
    send_weight = master[piece_expert].astype(jnp.bfloat16)
    recv_weight = lax.all_to_all(send_weight, "expert", split_axis=1, concat_axis=1, tiled=True)
    recv_x, recv_dh = (
        lax.all_to_all(send_x, "expert", split_axis=1, concat_axis=1, tiled=True),
        lax.all_to_all(send_dh, "expert", split_axis=1, concat_axis=1, tiled=True),
    )
    rows_x = recv_x.reshape(slot_local, expert_devices * MOST, model_width)
    rows_dh = recv_dh.reshape(slot_local, expert_devices * MOST, hidden_width)
    own_piece = recv_weight.reshape(slot_local, piece_rows, 2 * model_width)
    replica = lax.all_gather(own_piece, "dp", axis=1, tiled=True)
    replica_split = replica.reshape(slot_local, hidden_width, 2, model_width)
    both_values = jnp.einsum(
        "lrd,lcgd->lrgc", rows_x, replica_split, preferred_element_type=jnp.float32
    )
    gate_value = both_values[:, :, 0, :]
    up_value = both_values[:, :, 1, :]
    sigmoid_value = jax.nn.sigmoid(gate_value)
    activation = gate_value * sigmoid_value
    derivative = sigmoid_value * (1.0 + gate_value * (1.0 - sigmoid_value))
    d_gate = (rows_dh * up_value * derivative).astype(jnp.bfloat16)
    d_up = (rows_dh * activation).astype(jnp.bfloat16)
    d_both = jnp.stack([d_gate, d_up], axis=2)
    grad_block = jnp.einsum("lrgc,lrd->clgd", d_both, rows_x, preferred_element_type=jnp.float32)
    summed_rows = lax.psum_scatter(
        grad_block.reshape(lax.axis_size("dp") * piece_rows, slot_local, 2 * model_width).astype(
            jnp.bfloat16
        ),
        "dp",
        scatter_dimension=0,
        tiled=True,
    ).astype(jnp.float32)
    replica_grad = jnp.swapaxes(summed_rows, 0, 1)
    outgoing = replica_grad.reshape(slot_local, expert_devices, shard_width)
    incoming = lax.all_to_all(
        outgoing.astype(jnp.bfloat16), "expert", split_axis=1, concat_axis=1, tiled=True
    ).astype(outgoing.dtype)
    by_slot = jnp.swapaxes(incoming, 0, 1).reshape(slot_count, shard_width)
    grads = jnp.dot(
        slot_hot.T.astype(jnp.float32),
        by_slot,
        precision=lax.Precision.HIGHEST,
        preferred_element_type=jnp.float32,
    )
    new_master, new_first, new_second = adamw_update(master, first_moment, second_moment, grads)
    return (new_master, new_first, new_second, replica_grad)


def solution(mesh):
    return jax.shard_map(
        local,
        mesh=mesh,
        in_specs=(
            P(("dp", "expert"), None),
            P(("dp", "expert"), None, None),
            P(("dp", "expert"), None),
            P(),
            P(None, ("dp", "expert")),
            P(None, ("dp", "expert")),
            P(None, ("dp", "expert")),
        ),
        out_specs=(
            P(None, ("dp", "expert")),
            P(None, ("dp", "expert")),
            P(None, ("dp", "expert")),
            P("expert", "dp", None),
        ),
        check_vma=False,
    )
```

profile of v0, /device:TPU:2, one launch (start us, length us, event | category | flops | bytes accessed | tf_op | source)
XLA Modules:
  0.0 246.4 jit_solution(11199312595041048416)
XLA Ops:
  7.2 0.7 compare_select_fusion.6
  7.9 1.8 gather_fusion.2
  9.7 0.3 copy.75
  10.1 0.5 broadcast.312
  10.6 1.8 reduce.6
  12.4 29.0 %all_to_all.20 = bf16[64,2,768]{2,1,0:T(2,128)(2,1)S(1)} all-to-all(bf16[64,2,768]{2,1,0:T(2,128)(2,1)S(1)} %reshape.309), channel_id=1, replica_groups=mesh['expert'=64,'dp'=16] {'expert'}, dimensions={0} | all-to-all | bytes 393216 | tf_op jit(solution)/shard_map/all_to_all | solution.py:74
  41.4 0.1 reshape.310
  41.6 1.1 bitcast_reduce_fusion
  42.6 0.9 reshape.272
  43.9 0.2 reduce_window_sum.11
  44.1 0.1 convert_reduce_fusion.1
  44.2 0.2 convert_reduce_fusion
  44.3 0.1 and_select_fusion.1
  44.5 0.2 select_reduce_fusion.3
  44.7 0.2 select_reduce_fusion.2
  44.9 0.2 select_reduce_fusion
  45.0 0.1 reduce_sum.64
  45.2 0.2 fusion.8
  45.4 0.2 broadcast_in_dim.110
  45.6 2.0 gather_fusion.1
  47.7 0.1 gather.18
  47.8 0.1 copy.57
  47.9 1.0 select_bitcast_fusion.1
  48.9 5.9 %all-to-all-start.1 = ((bf16[1,64,5,384]{3,2,0,1:T(8,128)(2,1)}), bf16[1,64,5,384]{3,2,0,1:T(8,128)(2,1)}, u32[]{:S(2)}, u32[]{:S(2)}) async-start(bf16[1,64,5,384]{3,2,0,1:T(8,128)(2,1)} %select_bitcast_fusion.1), calls=%async_computation.1 | async-start | bytes 786432 | tf_op jit(solution)/shard_map/all_to_all | solution.py:77
  54.8 2.4 gather_fusion
  57.3 0.6 gather.16
  57.8 0.1 copy.53
  57.9 1.8 select_bitcast_fusion
  59.7 9.3 %all-to-all-done.1 = bf16[1,64,5,384]{3,2,0,1:T(8,128)(2,1)} async-done(((bf16[1,64,5,384]{3,2,0,1:T(8,128)(2,1)}), bf16[1,64,5,384]{3,2,0,1:T(8,128)(2,1)}, u32[]{:S(2)}, u32[]{:S(2)}) %all-to-all-start.1) | async-done | bytes 245792 | tf_op jit(solution)/shard_map/all_to_all | solution.py:77
  69.0 5.0 %all-to-all-start = ((bf16[1,64,5,2048]{3,2,0,1:T(8,128)(2,1)}), bf16[1,64,5,2048]{3,2,0,1:T(8,128)(2,1)S(1)}, u32[]{:S(2)}, u32[]{:S(2)}) async-start(bf16[1,64,5,2048]{3,2,0,1:T(8,128)(2,1)} %select_bitcast_fusion), calls=%async_computation | async-start | bytes 4194304 | tf_op jit(solution)/shard_map/all_to_all | solution.py:76
  74.0 0.2 reduce-scatter.2.cloned.1.call-start
  74.2 1.9 reshape.305
  76.1 45.0 %all-to-all-done = bf16[1,64,5,2048]{3,2,0,1:T(8,128)(2,1)S(1)} async-done(((bf16[1,64,5,2048]{3,2,0,1:T(8,128)(2,1)}), bf16[1,64,5,2048]{3,2,0,1:T(8,128)(2,1)S(1)}, u32[]{:S(2)}, u32[]{:S(2)}) %all-to-all-start) | async-done | bytes 1310752 | tf_op jit(solution)/shard_map/all_to_all | solution.py:76
  121.1 1.4 reshape.303
  122.5 3.4 %copy.60 = bf16[1,384,4096]{1,2,0:T(8,128)(2,1)S(1)} copy(bf16[1,384,4096]{2,1,0:T(8,128)(2,1)} %all-gather.2.cloned.1.call-done) | data formatting | bytes 6291456 | tf_op jit(solution)/shard_map/all_gather | solution.py:82
  125.9 2.6 %convolution_bitcast_fusion = f32[1,320,2,384]{3,1,2,0:T(8,128)S(1)} fusion(bf16[320,2048,1]{1,0,2:T(8,128)(2,1)} %reshape.303, bf16[384,2,2048]{0,2,1:T(8,128)(2,1)S(1)} %bitcast.47), kind=kOutput, calls=%fused_computation.5 | convolution fusion | flops 1006632960 | bytes 5439488 | tf_op jit(solution)/shard_map/lrd,lcgd->lrgc/dot_general | solution.py:84
  128.5 0.3 fusion.1
  128.9 1.8 convolution_convert_fusion
  130.7 2.9 %copy.64 = bf16[384,1,4096]{2,0,1:T(8,128)(2,1)} copy(bf16[384,1,4096]{0,2,1:T(8,128)(2,1)S(1)} %bitcast.46) | data formatting | bytes 6291456 | tf_op jit(solution)/shard_map/convert_element_type | solution.py:97
  133.7 75.5 %reduce-scatter.2.cloned.1.call-done = bf16[24,1,4096]{2,0,1:T(8,128)(2,1)} async-done(((bf16[384,1,4096]{2,0,1:T(8,128)(2,1)}), bf16[24,1,4096]{2,0,1:T(8,128)(2,1)}) %reduce-scatter.2.cloned.1.call-update) | async-done | bytes 196624 | tf_op jit(solution)/shard_map/reduce_scatter | solution.py:96
  209.2 1.3 convert_element_type.100
  210.5 1.8 reduce.7
  212.3 0.7 reshape.311
  213.0 12.8 %all-to-all-start.3 = ((bf16[64,2,768]{2,1,0:T(2,128)(2,1)}), bf16[64,2,768]{2,1,0:T(2,128)(2,1)S(1)}, u32[]{:S(2)}, u32[]{:S(2)}) async-start(bf16[64,2,768]{2,1,0:T(2,128)(2,1)} %reshape.311), calls=%async_computation.4 | async-start | bytes 393216 | tf_op jit(solution)/shard_map/all_to_all | solution.py:106
  225.8 0.8 bitcast_convert_fusion
  226.6 11.7 %all-to-all-done.3 = bf16[64,2,768]{2,1,0:T(2,128)(2,1)S(1)} async-done(((bf16[64,2,768]{2,1,0:T(2,128)(2,1)}), bf16[64,2,768]{2,1,0:T(2,128)(2,1)S(1)}, u32[]{:S(2)}, u32[]{:S(2)}) %all-to-all-start.3) | async-done | bytes 196640 | tf_op jit(solution)/shard_map/all_to_all | solution.py:106
  238.3 0.1 reshape.312
  238.5 1.1 multiply_subtract_fusion
  (34 shorter events, 0.6 us)
Async XLA Ops:
  7.2 38.4 %copy-start = (bf16[16,8,384]{2,1,0:T(8,128)(2,1)S(1)}, bf16[16,8,384]{2,1,0:T(8,128)(2,1)}, u32[]{:S(2)}) copy-start(bf16[16,8,384]{2,1,0:T(8,128)(2,1)} %param.8) | copy-start | bytes 294916
  7.2 115.3 %all-gather.2.cloned.1.call-start = ((), (), s32[]{:S(2)}) async-start(), calls=%async_computation.5 | async-start | bytes 3342336 | tf_op jit(solution)/shard_map/all_gather | solution.py:82
  9.7 33.9 %copy-start.6 = (s32[16,8]{0,1:T(8,128)S(1)}, s32[16,8]{0,1:T(8,128)}, u32[]{:S(2)}) copy-start(s32[16,8]{0,1:T(8,128)} %param.9) | copy-start | bytes 1540
  9.7 34.3 %copy-start.7 = (s32[64]{0:T(128)S(1)}, s32[64]{0:T(128)}, u32[]{:S(2)}) copy-start(s32[64]{0:T(128)} %param.10) | copy-start | bytes 772
  45.6 9.2 %copy-start.1 = (bf16[16,2048]{1,0:T(8,128)(2,1)S(1)}, bf16[16,2048]{1,0:T(8,128)(2,1)}, u32[]{:S(2)}) copy-start(bf16[16,2048]{1,0:T(8,128)(2,1)} %param.7) | copy-start | bytes 196612
  48.9 20.1 %all-to-all-start.1 = ((bf16[1,64,5,384]{3,2,0,1:T(8,128)(2,1)}), bf16[1,64,5,384]{3,2,0,1:T(8,128)(2,1)}, u32[]{:S(2)}, u32[]{:S(2)}) async-start(bf16[1,64,5,384]{3,2,0,1:T(8,128)(2,1)} %select_bitcast_fusion.1), calls=%async_computation.1 | async-start | bytes 786432 | tf_op jit(solution)/shard_map/all_to_all | solution.py:77
  69.0 52.1 %all-to-all-start = ((bf16[1,64,5,2048]{3,2,0,1:T(8,128)(2,1)}), bf16[1,64,5,2048]{3,2,0,1:T(8,128)(2,1)S(1)}, u32[]{:S(2)}, u32[]{:S(2)}) async-start(bf16[1,64,5,2048]{3,2,0,1:T(8,128)(2,1)} %select_bitcast_fusion), calls=%async_computation | async-start | bytes 4194304 | tf_op jit(solution)/shard_map/all_to_all | solution.py:76
  74.0 135.2 %reduce-scatter.2.cloned.1.call-start = ((), (), s32[]{:S(2)}) async-start(), calls=%async_computation.6 | async-start | bytes 3342336 | tf_op jit(solution)/shard_map/reduce_scatter | solution.py:96
  125.9 2.6 %copy-start.3 = (f32[1,320,1,384]{3,1,2,0:T(8,128)S(1)}, f32[1,320,1,384]{3,1,2,0:T(8,128)}, u32[]{:S(2)}) copy-start(f32[1,320,1,384]{3,1,2,0:T(8,128)} %reshape.305) | copy-start | bytes 1474564
  125.9 2.9 %copy-start.4 = (bf16[320,2048,1]{1,0,2:T(8,128)(2,1)S(1)}, bf16[320,2048,1]{1,0,2:T(8,128)(2,1)}, u32[]{:S(2)}) copy-start(bf16[320,2048,1]{1,0,2:T(8,128)(2,1)} %reshape.303) | copy-start | bytes 3932164
  133.6 104.8 %copy-start.2 = (f32[32,1536]{1,0:T(8,128)S(1)}, f32[32,1536]{1,0:T(8,128)}, u32[]{:S(2)}) copy-start(f32[32,1536]{1,0:T(8,128)} %param.11) | copy-start | bytes 589828
  133.6 104.8 %copy-start.8 = (f32[32,1536]{1,0:T(8,128)S(1)}, f32[32,1536]{1,0:T(8,128)}, u32[]{:S(2)}) copy-start(f32[32,1536]{1,0:T(8,128)} %param.12) | copy-start | bytes 589828
  133.7 104.8 %copy-start.9 = (f32[32,1536]{1,0:T(8,128)S(1)}, f32[32,1536]{1,0:T(8,128)}, u32[]{:S(2)}) copy-start(f32[32,1536]{1,0:T(8,128)} %param.13) | copy-start | bytes 589828
  209.2 16.6 %copy-start.5 = (bf16[24,1,4096]{2,0,1:T(8,128)(2,1)S(1)}, bf16[24,1,4096]{2,0,1:T(8,128)(2,1)}, u32[]{:S(2)}) copy-start(bf16[24,1,4096]{2,0,1:T(8,128)(2,1)} %reduce-scatter.2.cloned.1.call-done) | copy-start | bytes 589828
  213.0 25.3 %all-to-all-start.3 = ((bf16[64,2,768]{2,1,0:T(2,128)(2,1)}), bf16[64,2,768]{2,1,0:T(2,128)(2,1)S(1)}, u32[]{:S(2)}, u32[]{:S(2)}) async-start(bf16[64,2,768]{2,1,0:T(2,128)(2,1)} %reshape.311), calls=%async_computation.4 | async-start | bytes 393216 | tf_op jit(solution)/shard_map/all_to_all | solution.py:106
Sparse Core Ops, SparseCore 0:
  43.7 47.5 all-gather.1
  133.8 75.3 reduce-scatter.1
where the time goes:
time: 247 us; the launch traced here: 246 us
  waiting for transfers between devices  142 us (57%)
  blocking collectives  29 us (12%)
  starting transfers between devices  23.9 us (10%)
  local copies, waits for them, and re-layouts  22.6 us (9%)
  between operations  14.4 us (6%)
  other arithmetic  9.44 us (4%)
  matrix products  5.54 us (2%)
    reduce_scatter x1, waiting for transfers between devices, local(): lax.psum_scatter(grad_block.reshape(lax.axis_size('dp') * piece_rows, slo...  75.5 us
    all_to_all x1, waiting for transfers between devices, local(): lax.all_to_all(send_x, 'expert', split_axis=1, concat_axis=1, tiled=True)  45 us
    all_to_all x1, blocking collectives, local(): lax.all_to_all(send_weight, 'expert', split_axis=1, concat_axis=1, tiled=...  29 us
    all_to_all x1, starting transfers between devices, local(): lax.all_to_all(outgoing.astype(jnp.bfloat16), 'expert', split_axis=1, con...  12.8 us
    all_to_all x1, waiting for transfers between devices, local(): lax.all_to_all(outgoing.astype(jnp.bfloat16), 'expert', split_axis=1, con...  11.7 us
    all_to_all x1, waiting for transfers between devices, local(): lax.all_to_all(send_dh, 'expert', split_axis=1, concat_axis=1, tiled=True)  9.32 us
    all_to_all x1, starting transfers between devices, local(): lax.all_to_all(send_dh, 'expert', split_axis=1, concat_axis=1, tiled=True)  5.93 us
    all_to_all x1, starting transfers between devices, local(): lax.all_to_all(send_x, 'expert', split_axis=1, concat_axis=1, tiled=True)  4.99 us
  transfers between devices with their start and end apart: 5, of which 4 were waited for; matrix products, arithmetic and copies ran while one was open for 6% of the time, Pallas kernels for 0%

commit v1 on v0

v1 whole, which is shorter than its diff:
```python
import functools

import jax
import jax.numpy as jnp
from jax import lax
from jax.experimental import pallas as pl
from jax.experimental.pallas import tpu as pltpu
from jax.sharding import Mesh, PartitionSpec as P

MOST = 5
LANES = 128
CORES = 2


beta_first = 0.9
beta_second = 0.95
learning_rate = 0.01
decay_rate = 0.1
epsilon = 1e-08
adam_steps = 20.0


def adamw_update(master, first_moment, second_moment, grads):
    new_first = beta_first * first_moment + (1.0 - beta_first) * grads
    new_second = beta_second * second_moment + (1.0 - beta_second) * grads * grads
    corr_first = 1.0 - beta_first**adam_steps
    corr_second = 1.0 - beta_second**adam_steps
    update = (
        new_first / corr_first / (jnp.sqrt(new_second / corr_second) + epsilon)
        + decay_rate * master
    )
    return (master - learning_rate * update, new_first, new_second)


def grads_kernel(piece_rows, core, x_own, x_other, dh_own, dh_other, weights, out):
    f32, bf16 = jnp.float32, jnp.bfloat16
    units, width = weights.shape[0], weights.shape[1] // 2
    hidden = dh_own.shape[1]
    across = (((1,), (1,)), ((), ()))
    unit = lax.broadcasted_iota(jnp.int32, (units, hidden), 0)
    column = lax.broadcasted_iota(jnp.int32, (units, hidden), 1)
    piece = unit // piece_rows
    wanted = (piece * CORES + core[0]) * piece_rows + unit - piece * piece_rows
    choose = (column == wanted).astype(f32).astype(bf16)
    d_gates, d_ups = [], []
    for x_ref, dh_ref in ((x_own, dh_own), (x_other, dh_other)):
        rows = x_ref[...]
        dh = lax.dot_general(choose, dh_ref[...], across, preferred_element_type=f32)
        gate = lax.dot_general(weights[:, :width], rows, across, preferred_element_type=f32)
        up = lax.dot_general(weights[:, width:], rows, across, preferred_element_type=f32)
        sig = jax.nn.sigmoid(gate)
        d_gates.append((dh * up * (sig * (1.0 + gate * (1.0 - sig)))).astype(bf16))
        d_ups.append((dh * (gate * sig)).astype(bf16))
    tile = 512
    for half, parts in enumerate((d_gates, d_ups)):
        for start in range(0, width, tile):
            cols = slice(start, start + tile)
            total = jnp.dot(parts[0], x_own[:, cols], preferred_element_type=f32)
            total += jnp.dot(parts[1], x_other[:, cols], preferred_element_type=f32)
            out[:, half * width + start : half * width + start + tile] = total.astype(bf16)


def swiglu_grads(core, x_own, x_other, dh_own, dh_other, weights, piece_rows):
    vmem = pl.BlockSpec(memory_space=pltpu.VMEM)
    flops = 16 * x_own.shape[0] * weights.size // 2
    return pl.pallas_call(
        functools.partial(grads_kernel, piece_rows),
        out_shape=jax.ShapeDtypeStruct(weights.shape, jnp.bfloat16),
        in_specs=[pl.BlockSpec(memory_space=pltpu.SMEM)] + [vmem] * 5,
        out_specs=vmem,
        cost_estimate=pl.CostEstimate(flops=flops, bytes_accessed=8 << 20, transcendentals=0),
    )(core.reshape(1), x_own, x_other, dh_own, dh_other, weights)


def local(tokens, cotangent, expert_ids, placement, master, first_moment, second_moment):
    bf16, f32, i32 = jnp.bfloat16, jnp.float32, jnp.int32
    slots = lax.axis_size("expert")
    planes = lax.axis_size("z")
    source_index = lax.axis_index("expert")
    core = lax.axis_index("c")
    expert_count, shard_width = master.shape
    token_rows, width = tokens.shape
    top_count = expert_ids.shape[1]
    hidden = cotangent.shape[2]
    assigned = token_rows * top_count
    piece_rows = shard_width * slots // (2 * width)
    rows = slots * MOST
    expert_range = jnp.arange(expert_count, dtype=i32)
    slot_range = jnp.arange(slots, dtype=i32)

    slot_hot = placement[:, None] == expert_range[None, :]
    send_weight = jnp.dot(
        slot_hot.astype(bf16), master.astype(bf16), preferred_element_type=f32
    ).astype(bf16)
    send_weight = send_weight.reshape(slots, shard_width // LANES, LANES)
    recv_weight = lax.all_to_all(send_weight, "expert", split_axis=0, concat_axis=0, tiled=True)

    replicas = jnp.sum(slot_hot.astype(i32), axis=0)
    earlier_same = (slot_range[:, None] > slot_range[None, :]) & (
        placement[:, None] == placement[None, :]
    )
    slot_rank = jnp.sum(earlier_same.astype(i32), axis=1)
    wanted = jnp.mod(source_index, replicas)
    target_hot = slot_hot & (slot_rank[:, None] == wanted[None, :])
    target_slot = jnp.sum(jnp.where(target_hot, slot_range[:, None], 0), axis=0)
    flat_ids = expert_ids.reshape(assigned)
    expert_hot = flat_ids[:, None] == expert_range[None, :]
    copy_range = jnp.arange(assigned, dtype=i32)
    before = (copy_range[:, None] > copy_range[None, :]) & (flat_ids[:, None] == flat_ids[None, :])
    position = jnp.sum(before.astype(i32), axis=1)
    destination = jnp.sum(jnp.where(expert_hot, target_slot[None, :], 0), axis=1)
    send_row = destination * MOST + position
    row_match = jnp.arange(rows, dtype=i32)[:, None] == send_row[None, :]
    pick = row_match.astype(bf16)
    token_of = (copy_range[:, None] // top_count == jnp.arange(token_rows, dtype=i32)[None, :])
    token_pick = jnp.dot(pick, token_of.astype(bf16), preferred_element_type=f32).astype(bf16)
    send_x = jnp.dot(token_pick, tokens, preferred_element_type=f32).astype(bf16)
    send_dh = jnp.dot(
        pick, cotangent.reshape(assigned, hidden), preferred_element_type=f32
    ).astype(bf16)
    x_rows = MOST * width // LANES
    dh_rows = MOST * hidden // LANES
    spare = -(x_rows + dh_rows) % 16
    send = jnp.concatenate(
        [
            send_x.reshape(slots, x_rows, LANES),
            send_dh.reshape(slots, dh_rows, LANES),
            jnp.zeros((slots, spare, LANES), bf16),
        ],
        axis=1,
    )
    send, recv_weight = lax.optimization_barrier((send, recv_weight))
    recv = lax.all_to_all(send, "expert", split_axis=0, concat_axis=0, tiled=True)
    other = lax.ppermute(recv, "c", [(0, 1), (1, 0)])

    own_piece = recv_weight.reshape(piece_rows, 2 * width)
    replica = lax.all_gather(own_piece, "z", axis=0, tiled=True)

    group = MOST + 1

    def rows_of(block):
        wide = block.reshape(slots * group, width)
        dh = block[:, x_rows : x_rows + dh_rows].reshape(slots, MOST, hidden)
        dh = jnp.pad(dh, ((0, 0), (0, group - MOST), (0, 0))).reshape(slots * group, hidden)
        return wide, dh

    x_own, dh_own = rows_of(recv)
    x_other, dh_other = rows_of(other)
    grad_block = swiglu_grads(core, x_own, x_other, dh_own, dh_other, replica, piece_rows)
    summed = lax.psum_scatter(grad_block, "z", scatter_dimension=0, tiled=True)
    replica_grad = summed.astype(f32)[None]

    outgoing = summed.reshape(slots, shard_width // LANES, LANES)
    incoming = lax.all_to_all(outgoing, "expert", split_axis=0, concat_axis=0, tiled=True)
    grads = lax.dot_general(
        slot_hot.astype(bf16),
        incoming.reshape(slots, shard_width),
        (((0,), (0,)), ((), ())),
        preferred_element_type=f32,
    )
    new_master, new_first, new_second = adamw_update(master, first_moment, second_moment, grads)
    return (new_master, new_first, new_second, replica_grad)


def solution(mesh):
    slots, dp = mesh.shape["expert"], mesh.shape["dp"]
    split = Mesh(
        mesh.devices.reshape(slots, dp // CORES, CORES), ("expert", "z", "c")
    )
    shard = ("z", "c", "expert")
    return jax.shard_map(
        local,
        mesh=split,
        in_specs=(
            P(shard, None),
            P(shard, None, None),
            P(shard, None),
            P(),
            P(None, shard),
            P(None, shard),
            P(None, shard),
        ),
        out_specs=(
            P(None, shard),
            P(None, shard),
            P(None, shard),
            P("expert", ("z", "c"), None),
        ),
        check_vma=False,
    )
```

time: 247 us -> 195 us (0.79)
  waiting for transfers between devices: 142 us -> 107 us
  blocking collectives: 29 us -> 0 us
  starting transfers between devices: 23.9 us -> 39.8 us
  Pallas kernels: 0 us -> 7.85 us
  local copies, waits for them, and re-layouts: 22.6 us -> 15.1 us
  other arithmetic: 9.44 us -> 6.17 us
    reduce_scatter x1, waiting for transfers between devices: 75.5 us -> 45.7 us  [local(): summed = lax.psum_scatter(grad_block, 'z', scatter_dimension=0, tiled=True)]
    all_to_all x1 -> x0, blocking collectives: 29 us -> none  [local(): lax.all_to_all(send_weight, 'expert', split_axis=1, concat_axis=1, tiled=...]
    all_to_all x3, waiting for transfers between devices: 66 us -> 51.6 us  [the longest x1 35.2 us: local(): lax.all_to_all(send, 'expert', split_axis=0, concat_axis=0, tiled=True)]
    all_to_all x3, starting transfers between devices: 23.7 us -> 37.8 us  [the longest x1 17.2 us: local(): lax.all_to_all(send_weight, 'expert', split_axis=0, concat_axis=0, tiled=...]
    reshape x1 -> x11, local copies, waits for them, and re-layouts: 0.93 us -> 12.2 us  [the longest x2 4.11 us: rows_of(): wide = block.reshape(slots * group, width)]
    all_gather x1, waiting for transfers between devices: 0.01 us -> 9.67 us  [local(): replica = lax.all_gather(own_piece, 'z', axis=0, tiled=True)]
    pallas_call x0 -> x1, Pallas kernels: none -> 7.85 us  [swiglu_grads(): pl.pallas_call(functools.partial(grads_kernel, piece_rows), out_shape=jax...]
    gather x5 -> x0, local copies, waits for them, and re-layouts: 6.96 us -> none  [the longest x2 2.99 us: local(): gathered_x = jnp.take(tokens, source_copy // top_count, axis=0)]
  transfers between devices with their start and end apart: 5 -> 6, of which waited for: 4 -> 5; matrix products, arithmetic and copies ran while one was open for 6% -> 10% of each run, Pallas kernels for 0% -> 0%
where the time goes in v1:
time: 195 us; the launch traced here: 194 us
  waiting for transfers between devices  107 us (55%)
  starting transfers between devices  39.8 us (20%)
  local copies, waits for them, and re-layouts  15.1 us (8%)
  between operations  14.2 us (7%)
  Pallas kernels  7.85 us (4%)
  other arithmetic  6.17 us (3%)
  matrix products  4.15 us (2%)
    reduce_scatter x1, waiting for transfers between devices, local(): summed = lax.psum_scatter(grad_block, 'z', scatter_dimension=0, tiled=True)  45.7 us
    all_to_all x1, waiting for transfers between devices, local(): lax.all_to_all(send, 'expert', split_axis=0, concat_axis=0, tiled=True)  35.2 us
    all_to_all x1, starting transfers between devices, local(): lax.all_to_all(send_weight, 'expert', split_axis=0, concat_axis=0, tiled=...  17.2 us
    all_to_all x1, starting transfers between devices, local(): lax.all_to_all(outgoing, 'expert', split_axis=0, concat_axis=0, tiled=True)  12.9 us
    all_to_all x1, waiting for transfers between devices, local(): lax.all_to_all(outgoing, 'expert', split_axis=0, concat_axis=0, tiled=True)  11.3 us
    all_gather x1, waiting for transfers between devices, local(): replica = lax.all_gather(own_piece, 'z', axis=0, tiled=True)  9.67 us
    pallas_call x1, Pallas kernels, swiglu_grads(): pl.pallas_call(functools.partial(grads_kernel, piece_rows), out_shape=jax...  7.85 us
    all_to_all x1, starting transfers between devices, local(): lax.all_to_all(send, 'expert', split_axis=0, concat_axis=0, tiled=True)  7.78 us
  transfers between devices with their start and end apart: 6, of which 5 were waited for; matrix products, arithmetic and copies ran while one was open for 10% of the time, Pallas kernels for 0%

profile of v1, /device:TPU:2, one launch (start us, length us, event | category | flops | bytes accessed | tf_op | source)
XLA Modules:
  0.0 194.2 jit_solution(8359059745891611180)
XLA Ops:
  7.2 0.0 copy-start
  7.2 1.2 convolution_convert_fusion.1
  8.4 0.9 reshape.115
  9.3 17.2 %all-to-all-start = ((bf16[64,12,128]{2,1,0:T(8,128)(2,1)}), bf16[64,12,128]{2,1,0:T(8,128)(2,1)S(1)}, u32[]{:S(2)}, u32[]{:S(2)}) async-start(bf16[64,12,128]{2,1,0:T(8,128)(2,1)} %reshape.115), calls=%async_computation | async-start | bytes 524288 | tf_op jit(solution)/shard_map/all_to_all | solution.py:96
  26.5 0.9 convert_reduce_fusion.1
  27.4 0.8 convert_reduce_fusion.2
  28.2 0.8 copy.13
  28.9 0.1 eq.105
  29.0 0.2 convert_reduce_fusion
  29.2 0.1 and_select_fusion.1
  29.3 0.8 select_reduce_fusion.1
  30.2 0.1 select_reduce_fusion
  30.3 1.6 convolution_convert_fusion
  31.9 0.0 copy-done
  31.9 0.2 convolution_convert_fusion.2
  32.1 0.2 reshape.114
  32.3 0.6 reshape.112
  33.0 0.1 pad.11.clone
  33.0 1.5 maximum_maximum_fusion
  34.6 5.0 %all-to-all-done = bf16[64,12,128]{2,1,0:T(8,128)(2,1)S(1)} async-done(((bf16[64,12,128]{2,1,0:T(8,128)(2,1)}), bf16[64,12,128]{2,1,0:T(8,128)(2,1)S(1)}, u32[]{:S(2)}, u32[]{:S(2)}) %all-to-all-start) | async-done | bytes 196640 | tf_op jit(solution)/shard_map/all_to_all | solution.py:96
  39.6 7.8 %all-to-all-start.1 = ((bf16[64,96,128]{2,1,0:T(8,128)(2,1)}), bf16[64,96,128]{2,1,0:T(8,128)(2,1)S(1)}, u32[]{:S(2)}, u32[]{:S(2)}) async-start(bf16[64,96,128]{2,1,0:T(8,128)(2,1)} %maximum_maximum_fusion), calls=%async_computation.1 | async-start | bytes 3145728 | tf_op jit(solution)/shard_map/all_to_all | solution.py:133
  47.4 0.0 all-gather.2.cloned.1.call-start
  47.5 0.9 reshape.122
  48.4 0.0 all-gather.2.cloned.1.call-update
  48.4 0.0 reduce-scatter.2.cloned.1.call-start
  48.5 35.2 %all-to-all-done.1 = bf16[64,96,128]{2,1,0:T(8,128)(2,1)S(1)} async-done(((bf16[64,96,128]{2,1,0:T(8,128)(2,1)}), bf16[64,96,128]{2,1,0:T(8,128)(2,1)S(1)}, u32[]{:S(2)}, u32[]{:S(2)}) %all-to-all-start.1) | async-done | bytes 1572896 | tf_op jit(solution)/shard_map/all_to_all | solution.py:133
  83.7 1.9 collective-permute-start
  85.6 0.9 reshape.118
  86.5 1.8 pad.7
  88.3 1.8 reshape.119.dh_own
  90.1 2.0 %reshape.116.x_own = bf16[384,2048]{1,0:T(8,128)(2,1)} reshape(bf16[64,96,128]{2,1,0:T(8,128)(2,1)S(1)} %all-to-all-done.1) | data formatting | bytes 3145728 | tf_op jit(solution)/shard_map/reshape | solution.py:142
  92.1 0.0 collective-permute-done
  92.2 0.1 reshape.120
  92.3 0.1 pad.8
  92.4 0.8 reshape.121.dh_other
  93.2 2.1 %reshape.117.x_other = bf16[384,2048]{1,0:T(8,128)(2,1)} reshape(bf16[64,96,128]{2,1,0:T(8,128)(2,1)S(1)} %collective-permute-done) | data formatting | bytes 3145728 | tf_op jit(solution)/shard_map/reshape | solution.py:142
  95.3 9.7 %all-gather.2.cloned.1.call-done.weights = bf16[192,4096]{1,0:T(8,128)(2,1)} async-done(((bf16[24,4096]{1,0:T(8,128)(2,1)}), bf16[192,4096]{1,0:T(8,128)(2,1)}) %all-gather.2.cloned.1.call-update) | async-done | bytes 1572880 | tf_op jit(solution)/shard_map/all_gather | solution.py:137
  104.9 7.8 %shard_map.102 = bf16[192,4096]{1,0:T(8,128)(2,1)} custom-call(s32[1]{0:T(128)} %bitcast.core, bf16[384,2048]{1,0:T(8,128)(2,1)} %reshape.116.x_own, bf16[384,2048]{1,0:T(8,128)(2,1)} %reshape.117.x_other, bf16[384,384]{1,0:T(8,128)(2,1)} %reshape.119.dh_own, bf16[384,384]{1,0:T(8,128)(2,1)} %reshape.121.dh_other, ...), custom_call_target="tpu_custom_call" | custom-call | flops 2415919104 | bytes 8388608 | tf_op jit(solution)/shard_map/pallas_call | solution.py:66
  112.8 0.0 reduce-scatter.2.cloned.1.call-update
  112.8 45.7 %reduce-scatter.2.cloned.1.call-done = bf16[24,4096]{1,0:T(8,128)(2,1)} async-done(((bf16[192,4096]{1,0:T(8,128)(2,1)}), bf16[24,4096]{1,0:T(8,128)(2,1)}) %reduce-scatter.2.cloned.1.call-update) | async-done | bytes 196624 | tf_op jit(solution)/shard_map/reduce_scatter | solution.py:150
  158.5 1.9 reshape.123
  160.4 12.9 %all-to-all-start.2 = ((bf16[64,12,128]{2,1,0:T(8,128)(2,1)}), bf16[64,12,128]{2,1,0:T(8,128)(2,1)S(1)}, u32[]{:S(2)}, u32[]{:S(2)}) async-start(bf16[64,12,128]{2,1,0:T(8,128)(2,1)} %reshape.123), calls=%async_computation.3 | async-start | bytes 524288 | tf_op jit(solution)/shard_map/all_to_all | solution.py:154
  173.3 1.7 bitcast_convert_fusion
  175.0 11.3 %all-to-all-done.2 = bf16[64,12,128]{2,1,0:T(8,128)(2,1)S(1)} async-done(((bf16[64,12,128]{2,1,0:T(8,128)(2,1)}), bf16[64,12,128]{2,1,0:T(8,128)(2,1)S(1)}, u32[]{:S(2)}, u32[]{:S(2)}) %all-to-all-start.2) | async-done | bytes 196640 | tf_op jit(solution)/shard_map/all_to_all | solution.py:154
  186.3 0.0 copy-done.1
  186.3 0.0 copy-done.2
  186.3 0.0 copy-done.4
  186.3 1.1 multiply_subtract_fusion
  (8 shorter events, 0.1 us)
Async XLA Ops:
  7.2 24.8 %copy-start = (bf16[16,8,384]{2,1,0:T(8,128)(2,1)S(1)}, bf16[16,8,384]{2,1,0:T(8,128)(2,1)}, u32[]{:S(2)}) copy-start(bf16[16,8,384]{2,1,0:T(8,128)(2,1)} %param.8) | copy-start | bytes 294916
  9.3 30.4 %all-to-all-start = ((bf16[64,12,128]{2,1,0:T(8,128)(2,1)}), bf16[64,12,128]{2,1,0:T(8,128)(2,1)S(1)}, u32[]{:S(2)}, u32[]{:S(2)}) async-start(bf16[64,12,128]{2,1,0:T(8,128)(2,1)} %reshape.115), calls=%async_computation | async-start | bytes 524288 | tf_op jit(solution)/shard_map/all_to_all | solution.py:96
  39.6 44.0 %all-to-all-start.1 = ((bf16[64,96,128]{2,1,0:T(8,128)(2,1)}), bf16[64,96,128]{2,1,0:T(8,128)(2,1)S(1)}, u32[]{:S(2)}, u32[]{:S(2)}) async-start(bf16[64,96,128]{2,1,0:T(8,128)(2,1)} %maximum_maximum_fusion), calls=%async_computation.1 | async-start | bytes 3145728 | tf_op jit(solution)/shard_map/all_to_all | solution.py:133
  47.4 57.5 %all-gather.2.cloned.1.call-start = ((), (), s32[]{:S(2)}) async-start(), calls=%async_computation.4 | async-start | bytes 1769472 | tf_op jit(solution)/shard_map/all_gather | solution.py:137
  48.4 110.1 %reduce-scatter.2.cloned.1.call-start = ((), (), s32[]{:S(2)}) async-start(), calls=%async_computation.5 | async-start | bytes 1769472 | tf_op jit(solution)/shard_map/reduce_scatter | solution.py:150
  83.7 8.5 %collective-permute-start = (bf16[64,96,128]{2,1,0:T(8,128)(2,1)S(1)}, bf16[64,96,128]{2,1,0:T(8,128)(2,1)S(1)}, u32[]{:S(2)}, u32[]{:S(2)}) collective-permute-start(bf16[64,96,128]{2,1,0:T(8,128)(2,1)S(1)} %all-to-all-done.1), channel_id=1, source_target_pairs={{0,1},{1,0},{2,3},{3,2},{4,5},{5,4},{6,7},{7,6},{8,9},{9,8},{10,11... | collective-permute-start | bytes 4718600 | tf_op jit(solution)/shard_map/ppermute | solution.py:134
  112.8 73.5 %copy-start.1 = (f32[32,1536]{1,0:T(8,128)S(1)}, f32[32,1536]{1,0:T(8,128)}, u32[]{:S(2)}) copy-start(f32[32,1536]{1,0:T(8,128)} %param.11) | copy-start | bytes 589828
  112.8 73.5 %copy-start.2 = (s32[64]{0:T(128)S(1)}, s32[64]{0:T(128)}, u32[]{:S(2)}) copy-start(s32[64]{0:T(128)} %param.10) | copy-start | bytes 772
  112.8 73.5 %copy-start.3 = (f32[32,1536]{1,0:T(8,128)S(1)}, f32[32,1536]{1,0:T(8,128)}, u32[]{:S(2)}) copy-start(f32[32,1536]{1,0:T(8,128)} %param.12) | copy-start | bytes 589828
  112.8 73.5 %copy-start.4 = (f32[32,1536]{1,0:T(8,128)S(1)}, f32[32,1536]{1,0:T(8,128)}, u32[]{:S(2)}) copy-start(f32[32,1536]{1,0:T(8,128)} %param.13) | copy-start | bytes 589828
  160.4 25.9 %all-to-all-start.2 = ((bf16[64,12,128]{2,1,0:T(8,128)(2,1)}), bf16[64,12,128]{2,1,0:T(8,128)(2,1)S(1)}, u32[]{:S(2)}, u32[]{:S(2)}) async-start(bf16[64,12,128]{2,1,0:T(8,128)(2,1)} %reshape.123), calls=%async_computation.3 | async-start | bytes 524288 | tf_op jit(solution)/shard_map/all_to_all | solution.py:154
Sparse Core Ops, SparseCore 0:
  51.5 53.4 all-gather.1
  113.0 45.5 reduce-scatter.1

commit v2 on v1

--- a/solution.py
+++ b/solution.py
@@ -6,6 +6,7 @@
 from jax.experimental import pallas as pl
 from jax.experimental.pallas import tpu as pltpu
 from jax.sharding import Mesh, PartitionSpec as P
+
 
 MOST = 5
 LANES = 128
@@ -32,22 +33,47 @@
     return (master - learning_rate * update, new_first, new_second)
 
 
-def grads_kernel(piece_rows, core, x_own, x_other, dh_own, dh_other, weights, out):
+def offset_of(block):
+    return jnp.where(block % 2 == 1, (block + 1) // 2, -(block // 2))
+
+
+def grads_kernel(planes, piece_rows, place, x_own, x_other, *refs):
     f32, bf16 = jnp.float32, jnp.bfloat16
+    pieces, out, weights = refs[:planes], refs[planes], refs[planes + 1]
     units, width = weights.shape[0], weights.shape[1] // 2
-    hidden = dh_own.shape[1]
+    hidden = units * CORES
+    for at, piece in enumerate(pieces):
+        weights[at * piece_rows : (at + 1) * piece_rows, :] = piece[...]
+    rows = x_own.shape[0]
+    sources = rows // (MOST + 1)
     across = (((1,), (1,)), ((), ()))
-    unit = lax.broadcasted_iota(jnp.int32, (units, hidden), 0)
-    column = lax.broadcasted_iota(jnp.int32, (units, hidden), 1)
-    piece = unit // piece_rows
-    wanted = (piece * CORES + core[0]) * piece_rows + unit - piece * piece_rows
-    choose = (column == wanted).astype(f32).astype(bf16)
+
+    def iota(shape, dim):
+        return lax.broadcasted_iota(jnp.int32, shape, dim)
+
+    def hot(mask):
+        return mask.astype(f32).astype(bf16)
+
+    unit = iota((units, hidden), 0)
+    block = unit // piece_rows
+    plane = place[0] + offset_of(block) + planes
+    plane = jnp.where(plane >= planes, plane - planes, plane)
+    plane = jnp.where(plane >= planes, plane - planes, plane)
+    column = (plane * CORES + place[1]) * piece_rows + unit - block * piece_rows
+    choose = hot(iota((units, hidden), 1) == column)
+    last = hot(iota((sources, rows), 1) == iota((sources, rows), 0) * (MOST + 1) + MOST)
     d_gates, d_ups = [], []
-    for x_ref, dh_ref in ((x_own, dh_own), (x_other, dh_other)):
-        rows = x_ref[...]
-        dh = lax.dot_general(choose, dh_ref[...], across, preferred_element_type=f32)
-        gate = lax.dot_general(weights[:, :width], rows, across, preferred_element_type=f32)
-        up = lax.dot_general(weights[:, width:], rows, across, preferred_element_type=f32)
+    for x_ref in (x_own, x_other):
+        packed = jnp.dot(last, x_ref[:, : MOST * hidden], preferred_element_type=f32).astype(bf16)
+        dh = jnp.zeros((units, rows), f32)
+        for at in range(MOST):
+            mine = packed[:, at * hidden : (at + 1) * hidden]
+            mine = lax.dot_general(choose, mine, across, preferred_element_type=f32).astype(bf16)
+            spread = hot(iota((sources, rows), 1) == iota((sources, rows), 0) * (MOST + 1) + at)
+            dh += jnp.dot(mine, spread, preferred_element_type=f32)
+        values = x_ref[...]
+        gate = lax.dot_general(weights[:, :width], values, across, preferred_element_type=f32)
+        up = lax.dot_general(weights[:, width:], values, across, preferred_element_type=f32)
         sig = jax.nn.sigmoid(gate)
         d_gates.append((dh * up * (sig * (1.0 + gate * (1.0 - sig)))).astype(bf16))
         d_ups.append((dh * (gate * sig)).astype(bf16))
@@ -60,16 +86,62 @@
             out[:, half * width + start : half * width + start + tile] = total.astype(bf16)
 
 
-def swiglu_grads(core, x_own, x_other, dh_own, dh_other, weights, piece_rows):
+def swiglu_grads(planes, piece_rows, place, x_own, x_other, pieces):
     vmem = pl.BlockSpec(memory_space=pltpu.VMEM)
-    flops = 16 * x_own.shape[0] * weights.size // 2
+    shape = (planes * piece_rows, pieces[0].shape[1])
+    flops = 8 * x_own.shape[0] * shape[0] * shape[1]
     return pl.pallas_call(
-        functools.partial(grads_kernel, piece_rows),
-        out_shape=jax.ShapeDtypeStruct(weights.shape, jnp.bfloat16),
-        in_specs=[pl.BlockSpec(memory_space=pltpu.SMEM)] + [vmem] * 5,
+        functools.partial(grads_kernel, planes, piece_rows),
+        out_shape=jax.ShapeDtypeStruct(shape, jnp.bfloat16),
+        in_specs=[pl.BlockSpec(memory_space=pltpu.SMEM)] + [vmem] * (2 + planes),
         out_specs=vmem,
+        scratch_shapes=[pltpu.VMEM(shape, jnp.bfloat16)],
         cost_estimate=pl.CostEstimate(flops=flops, bytes_accessed=8 << 20, transcendentals=0),
-    )(core.reshape(1), x_own, x_other, dh_own, dh_other, weights)
+    )(place, x_own, x_other, *pieces)
+
+
+def shift(value, planes, by):
+    return lax.ppermute(value, "z", [(i, (i - by) % planes) for i in range(planes)])
+
+
+def shift_by_core(value, planes, by):
+    pairs = []
+    for i in range(planes):
+        pairs.append((i * CORES, (i - by) % planes * CORES))
+        pairs.append((i * CORES + 1, (i + by) % planes * CORES + 1))
+    return lax.ppermute(value, ("z", "c"), pairs)
+
+
+def gather_planes(piece, planes):
+    pieces = [piece]
+    for by in range(1, planes // 2):
+        pieces += [shift(piece, planes, by), shift(piece, planes, -by)]
+    return pieces + [shift(piece, planes, planes // 2)]
+
+
+def scatter_planes(blocks, planes, core):
+    f32 = jnp.float32
+    own, up1, down1, up2, down2, up3, down3, far = blocks
+    more_up1, more_down1 = shift(up3, planes, -2), shift(down3, planes, 2)
+    more_far = shift_by_core(far, planes, -2).astype(f32)
+    first = core == 0
+
+    def add(value, more):
+        return (value.astype(f32) + more).astype(value.dtype)
+
+    up1, down1 = add(up1, more_up1.astype(f32)), add(down1, more_down1.astype(f32))
+    up2 = add(up2, jnp.where(first, more_far, 0.0))
+    down2 = add(down2, jnp.where(first, 0.0, more_far))
+    parts = [
+        shift(up1, planes, -1),
+        shift(down1, planes, 1),
+        shift(up2, planes, -2),
+        shift(down2, planes, 2),
+    ]
+    total = own.astype(f32)
+    for part in parts:
+        total = total + part.astype(f32)
+    return total
 
 
 def local(tokens, cotangent, expert_ids, placement, master, first_moment, second_moment):
@@ -134,24 +206,25 @@
     other = lax.ppermute(recv, "c", [(0, 1), (1, 0)])
 
     own_piece = recv_weight.reshape(piece_rows, 2 * width)
-    replica = lax.all_gather(own_piece, "z", axis=0, tiled=True)
+    pieces = gather_planes(own_piece, planes)
 
     group = MOST + 1
-
-    def rows_of(block):
-        wide = block.reshape(slots * group, width)
-        dh = block[:, x_rows : x_rows + dh_rows].reshape(slots, MOST, hidden)
-        dh = jnp.pad(dh, ((0, 0), (0, group - MOST), (0, 0))).reshape(slots * group, hidden)
-        return wide, dh
-
-    x_own, dh_own = rows_of(recv)
-    x_other, dh_other = rows_of(other)
-    grad_block = swiglu_grads(core, x_own, x_other, dh_own, dh_other, replica, piece_rows)
-    summed = lax.psum_scatter(grad_block, "z", scatter_dimension=0, tiled=True)
-    replica_grad = summed.astype(f32)[None]
-
-    outgoing = summed.reshape(slots, shard_width // LANES, LANES)
+    place = jnp.stack([lax.axis_index("z"), core])
+    grad_block = swiglu_grads(
+        planes,
+        piece_rows,
+        place,
+        recv.reshape(slots * group, width),
+        other.reshape(slots * group, width),
+        pieces,
+    )
+    blocks = [grad_block[k * piece_rows : (k + 1) * piece_rows] for k in range(planes)]
+    summed = scatter_planes(blocks, planes, core)
+    replica_grad = summed[None]
+
+    outgoing = summed.astype(bf16).reshape(slots, shard_width // LANES, LANES)
     incoming = lax.all_to_all(outgoing, "expert", split_axis=0, concat_axis=0, tiled=True)
+    incoming, replica_grad = lax.optimization_barrier((incoming, replica_grad))
     grads = lax.dot_general(
         slot_hot.astype(bf16),
         incoming.reshape(slots, shard_width),

time: 195 us -> 216 us (1.11)
  waiting for transfers between devices: 107 us -> 33.3 us
  blocking collectives: 0 us -> 62.6 us
  starting transfers between devices: 39.8 us -> 87.8 us
  between operations: 14.2 us -> 0.98 us
  local copies, waits for them, and re-layouts: 15.1 us -> 9.1 us
    ppermute x0 -> x14, starting transfers between devices: none -> 68.6 us  [the longest x13 66.7 us: shift(): lax.ppermute(value, 'z', [(i, (i - by) % planes) for i in range(planes)])]
    all_to_all x0 -> x2, blocking collectives: none -> 62.6 us  [the longest x1 42.7 us: local(): lax.all_to_all(send, 'expert', split_axis=0, concat_axis=0, tiled=True)]
    all_to_all x2 -> x0, waiting for transfers between devices: 46.5 us -> none  [the longest x1 35.2 us: local(): lax.all_to_all(send, 'expert', split_axis=0, concat_axis=0, tiled=True)]
    reduce_scatter x1 -> x0, waiting for transfers between devices: 45.7 us -> none  [local(): summed = lax.psum_scatter(grad_block, 'z', scatter_dimension=0, tiled=True)]
    ppermute x0 -> x14, waiting for transfers between devices: none -> 27.1 us  [the longest x13 20.5 us: shift(): lax.ppermute(value, 'z', [(i, (i - by) % planes) for i in range(planes)])]
    all_to_all x2 -> x0, starting transfers between devices: 20.6 us -> none  [the longest x1 12.9 us: local(): lax.all_to_all(outgoing, 'expert', split_axis=0, concat_axis=0, tiled=True)]
    all_gather x1 -> x0, waiting for transfers between devices: 9.67 us -> none  [local(): replica = lax.all_gather(own_piece, 'z', axis=0, tiled=True)]
    reshape x7 -> x3, local copies, waits for them, and re-layouts: 9.61 us -> 4.4 us  [the longest x1 2.08 us: local(): recv.reshape(slots * group, width)]
  transfers between devices with their start and end apart: 6 -> 16, of which waited for: 5 -> 10; matrix products, arithmetic and copies ran while one was open for 10% -> 6% of each run, Pallas kernels for 0% -> 0%
where the time goes in v2:
time: 216 us; the launch traced here: 215 us
  starting transfers between devices  87.8 us (41%)
  blocking collectives  62.6 us (29%)
  waiting for transfers between devices  33.3 us (15%)
  Pallas kernels  9.69 us (4%)
  local copies, waits for them, and re-layouts  9.1 us (4%)
  other arithmetic  7.14 us (3%)
  matrix products  4.15 us (2%)
    ppermute x13, starting transfers between devices, shift(): lax.ppermute(value, 'z', [(i, (i - by) % planes) for i in range(planes)])  66.7 us
    all_to_all x1, blocking collectives, local(): lax.all_to_all(send, 'expert', split_axis=0, concat_axis=0, tiled=True)  42.7 us
    ppermute x13, waiting for transfers between devices, shift(): lax.ppermute(value, 'z', [(i, (i - by) % planes) for i in range(planes)])  20.5 us
    all_to_all x1, blocking collectives, local(): lax.all_to_all(outgoing, 'expert', split_axis=0, concat_axis=0, tiled=True)  19.9 us
    all_to_all x1, starting transfers between devices, local(): lax.all_to_all(send_weight, 'expert', split_axis=0, concat_axis=0, tiled=...  17.2 us
    pallas_call x1, Pallas kernels, swiglu_grads(): pl.pallas_call(functools.partial(grads_kernel, planes, piece_rows), out_s...  9.69 us
    ppermute x1, waiting for transfers between devices, shift_by_core(): return lax.ppermute(value, ('z', 'c'), pairs)  6.6 us
    all_to_all x1, waiting for transfers between devices, local(): lax.all_to_all(send_weight, 'expert', split_axis=0, concat_axis=0, tiled=...  6.2 us
  transfers between devices with their start and end apart: 16, of which 10 were waited for; matrix products, arithmetic and copies ran while one was open for 6% of the time, Pallas kernels for 0%

profile of v2, /device:TPU:2, one launch (start us, length us, event | category | flops | bytes accessed | tf_op | source)
XLA Modules:
  0.0 214.7 jit_solution(9964023413863010889)
XLA Ops:
  0.6 1.2 convolution_convert_fusion.1
  1.9 0.9 reshape.99
  2.7 17.2 %all-to-all-start = ((bf16[64,12,128]{2,1,0:T(8,128)(2,1)}), bf16[64,12,128]{2,1,0:T(8,128)(2,1)S(1)}, u32[]{:S(2)}, u32[]{:S(2)}) async-start(bf16[64,12,128]{2,1,0:T(8,128)(2,1)} %reshape.99), calls=%async_computation | async-start | bytes 524288 | tf_op jit(solution)/shard_map/all_to_all | solution.py:168
  20.0 0.8 convert_reduce_fusion.2
  20.7 0.9 convert_reduce_fusion.1
  21.6 0.8 copy.13
  22.5 0.2 convert_reduce_fusion
  22.8 0.8 select_reduce_fusion.1
  23.7 1.6 convolution_convert_fusion
  25.4 0.6 reshape.96
  26.0 0.2 convolution_convert_fusion.2
  26.5 0.4 maximum_maximum_fusion
  26.9 6.2 %all-to-all-done = bf16[64,12,128]{2,1,0:T(8,128)(2,1)S(1)} async-done(((bf16[64,12,128]{2,1,0:T(8,128)(2,1)}), bf16[64,12,128]{2,1,0:T(8,128)(2,1)S(1)}, u32[]{:S(2)}, u32[]{:S(2)}) %all-to-all-start) | async-done | bytes 196640 | tf_op jit(solution)/shard_map/all_to_all | solution.py:168
  33.1 42.7 %all_to_all.15 = bf16[64,96,128]{2,1,0:T(8,128)(2,1)S(1)} all-to-all(bf16[64,96,128]{2,1,0:T(8,128)(2,1)S(1)} %maximum_maximum_fusion), channel_id=1, replica_groups=mesh['expert'=64,'z'=8,'c'=2] {'expert'}, dimensions={0} | all-to-all | bytes 3145728 | tf_op jit(solution)/shard_map/all_to_all | solution.py:205
  75.8 1.9 collective-permute-start
  77.7 0.9 reshape.102.refs_0_
  78.6 17.5 %collective-permute-start.1 = (bf16[24,4096]{1,0:T(8,128)(2,1)}, bf16[24,4096]{1,0:T(8,128)(2,1)S(1)}, u32[]{:S(2)}, u32[]{:S(2)}) collective-permute-start(bf16[24,4096]{1,0:T(8,128)(2,1)} %reshape.102.refs_0_), channel_id=1, source_target_pairs={{0,14},{2,0},{4,2},{6,4},{8,6},{10,8},{12,10},{14,12},{1,15},{3,1}... | collective-permute-start | bytes 589832 | tf_op jit(solution)/shard_map/ppermute | solution.py:104
  96.1 1.9 collective-permute-start.2
  98.1 3.4 %collective-permute-start.3 = (bf16[24,4096]{1,0:T(8,128)(2,1)}, bf16[24,4096]{1,0:T(8,128)(2,1)}, u32[]{:S(2)}, u32[]{:S(2)}) collective-permute-start(bf16[24,4096]{1,0:T(8,128)(2,1)} %reshape.102.refs_0_), channel_id=1, source_target_pairs={{0,12},{2,14},{4,0},{6,2},{8,4},{10,6},{12,8},{14,10},{1,13},{3,15... | collective-permute-start | bytes 589832 | tf_op jit(solution)/shard_map/ppermute | solution.py:104
  101.4 3.4 %collective-permute-start.4 = (bf16[24,4096]{1,0:T(8,128)(2,1)}, bf16[24,4096]{1,0:T(8,128)(2,1)}, u32[]{:S(2)}, u32[]{:S(2)}) collective-permute-start(bf16[24,4096]{1,0:T(8,128)(2,1)} %reshape.102.refs_0_), channel_id=1, source_target_pairs={{0,4},{2,6},{4,8},{6,10},{8,12},{10,14},{12,0},{14,2},{1,5},{3,7},... | collective-permute-start | bytes 589832 | tf_op jit(solution)/shard_map/ppermute | solution.py:104
  104.9 4.6 %collective-permute-start.5 = (bf16[24,4096]{1,0:T(8,128)(2,1)}, bf16[24,4096]{1,0:T(8,128)(2,1)}, u32[]{:S(2)}, u32[]{:S(2)}) collective-permute-start(bf16[24,4096]{1,0:T(8,128)(2,1)} %reshape.102.refs_0_), channel_id=1, source_target_pairs={{0,10},{2,12},{4,14},{6,0},{8,2},{10,4},{12,6},{14,8},{1,11},{3,13... | collective-permute-start | bytes 589832 | tf_op jit(solution)/shard_map/ppermute | solution.py:104
  109.5 3.1 %collective-permute-start.6 = (bf16[24,4096]{1,0:T(8,128)(2,1)}, bf16[24,4096]{1,0:T(8,128)(2,1)}, u32[]{:S(2)}, u32[]{:S(2)}) collective-permute-start(bf16[24,4096]{1,0:T(8,128)(2,1)} %reshape.102.refs_0_), channel_id=1, source_target_pairs={{0,6},{2,8},{4,10},{6,12},{8,14},{10,0},{12,2},{14,4},{1,7},{3,9},... | collective-permute-start | bytes 589832 | tf_op jit(solution)/shard_map/ppermute | solution.py:104
  112.6 5.8 %collective-permute-start.7 = (bf16[24,4096]{1,0:T(8,128)(2,1)}, bf16[24,4096]{1,0:T(8,128)(2,1)}, u32[]{:S(2)}, u32[]{:S(2)}) collective-permute-start(bf16[24,4096]{1,0:T(8,128)(2,1)} %reshape.102.refs_0_), channel_id=1, source_target_pairs={{0,8},{2,10},{4,12},{6,14},{8,0},{10,2},{12,4},{14,6},{1,9},{3,11}... | collective-permute-start | bytes 589832 | tf_op jit(solution)/shard_map/ppermute | solution.py:104
  118.4 0.6 pad_add_fusion.place
  119.0 2.1 reshape.100.x_own
  121.1 2.1 reshape.101.x_other
  123.1 1.7 collective-permute-done.5.refs_5_
  124.8 4.0 %collective-permute-done.6.refs_6_ = bf16[24,4096]{1,0:T(8,128)(2,1)} collective-permute-done((bf16[24,4096]{1,0:T(8,128)(2,1)}, bf16[24,4096]{1,0:T(8,128)(2,1)}, u32[]{:S(2)}, u32[]{:S(2)}) %collective-permute-start.6) | collective-permute-done | bytes 196640 | tf_op jit(solution)/shard_map/ppermute | solution.py:104
  128.8 7.1 %collective-permute-done.7.refs_7_ = bf16[24,4096]{1,0:T(8,128)(2,1)} collective-permute-done((bf16[24,4096]{1,0:T(8,128)(2,1)}, bf16[24,4096]{1,0:T(8,128)(2,1)}, u32[]{:S(2)}, u32[]{:S(2)}) %collective-permute-start.7) | collective-permute-done | bytes 196640 | tf_op jit(solution)/shard_map/ppermute | solution.py:104
  135.9 9.7 %shard_map.102 = bf16[192,4096]{1,0:T(8,128)(2,1)} custom-call(s32[2]{0:T(128)} %pad_add_fusion.place, bf16[384,2048]{1,0:T(8,128)(2,1)} %reshape.100.x_own, bf16[384,2048]{1,0:T(8,128)(2,1)} %reshape.101.x_other, bf16[24,4096]{1,0:T(8,128)(2,1)} %reshape.102.refs_0_, bf16[24,4096]{1,0:T(8,128)(2,1)} %copy-done.5, bf16[24,4096]{1,0:T(8,128)(2,1)} %copy-done.6, ...), custom_call_target="tpu_custom_call" | custom-call | flops 2415919104 | bytes 8388608 | tf_op jit(solution)/shard_map/pallas_call | solution.py:93
  145.6 1.2 fusion.23
  146.8 7.1 %collective-permute-start.10 = (bf16[24,4096]{1,0:T(8,128)(2,1)S(1)}, bf16[24,4096]{1,0:T(8,128)(2,1)S(1)}, u32[]{:S(2)}, u32[]{:S(2)}) collective-permute-start(bf16[24,4096]{1,0:T(8,128)(2,1)S(1)} %get-tuple-element.22), channel_id=1, source_target_pairs={{0,12},{2,14},{4,0},{6,2},{8,4},{10,6},{12,8},{14,10},{1,13},{3,15... | collective-permute-start | bytes 589832 | tf_op jit(solution)/shard_map/ppermute | solution.py:104
  153.9 1.9 collective-permute-start.12
  155.8 6.0 %collective-permute-start.8 = (bf16[24,4096]{1,0:T(8,128)(2,1)S(1)}, bf16[24,4096]{1,0:T(8,128)(2,1)S(1)}, u32[]{:S(2)}, u32[]{:S(2)}) collective-permute-start(bf16[24,4096]{1,0:T(8,128)(2,1)S(1)} %get-tuple-element.20), channel_id=1, source_target_pairs={{0,4},{2,6},{4,8},{6,10},{8,12},{10,14},{12,0},{14,2},{1,5},{3,7},... | collective-permute-start | bytes 589832 | tf_op jit(solution)/shard_map/ppermute | solution.py:104
  162.0 6.6 %collective-permute-done.12 = bf16[24,4096]{1,0:T(8,128)(2,1)S(1)} collective-permute-done((bf16[24,4096]{1,0:T(8,128)(2,1)S(1)}, bf16[24,4096]{1,0:T(8,128)(2,1)S(1)}, u32[]{:S(2)}, u32[]{:S(2)}) %collective-permute-start.12) | collective-permute-done | bytes 196640 | tf_op jit(solution)/shard_map/ppermute | solution.py:112
  168.6 2.2 %collective-permute-done.8 = bf16[24,4096]{1,0:T(8,128)(2,1)S(1)} collective-permute-done((bf16[24,4096]{1,0:T(8,128)(2,1)S(1)}, bf16[24,4096]{1,0:T(8,128)(2,1)S(1)}, u32[]{:S(2)}, u32[]{:S(2)}) %collective-permute-start.8) | collective-permute-done | bytes 196640 | tf_op jit(solution)/shard_map/ppermute | solution.py:104
  170.8 1.4 fusion.1
  172.3 2.2 %collective-permute-start.11 = (bf16[24,4096]{1,0:T(8,128)(2,1)S(1)}, bf16[24,4096]{1,0:T(8,128)(2,1)S(1)}, u32[]{:S(2)}, u32[]{:S(2)}) collective-permute-start(bf16[24,4096]{1,0:T(8,128)(2,1)S(1)} %get-tuple-element.23), channel_id=1, source_target_pairs={{0,14},{2,0},{4,2},{6,4},{8,6},{10,8},{12,10},{14,12},{1,15},{3,1}... | collective-permute-start | bytes 589832 | tf_op jit(solution)/shard_map/ppermute | solution.py:104
  174.5 5.3 %collective-permute-start.13 = (bf16[24,4096]{1,0:T(8,128)(2,1)S(1)}, bf16[24,4096]{1,0:T(8,128)(2,1)S(1)}, u32[]{:S(2)}, u32[]{:S(2)}) collective-permute-start(bf16[24,4096]{1,0:T(8,128)(2,1)S(1)} %get-tuple-element.17), channel_id=1, source_target_pairs={{0,4},{2,6},{4,8},{6,10},{8,12},{10,14},{12,0},{14,2},{1,5},{3,7},... | collective-permute-start | bytes 589832 | tf_op jit(solution)/shard_map/ppermute | solution.py:104
  179.7 2.7 %collective-permute-start.14 = (bf16[24,4096]{1,0:T(8,128)(2,1)S(1)}, bf16[24,4096]{1,0:T(8,128)(2,1)S(1)}, u32[]{:S(2)}, u32[]{:S(2)}) collective-permute-start(bf16[24,4096]{1,0:T(8,128)(2,1)S(1)} %get-tuple-element.18), channel_id=1, source_target_pairs={{0,12},{2,14},{4,0},{6,2},{8,4},{10,6},{12,8},{14,10},{1,13},{3,15... | collective-permute-start | bytes 589832 | tf_op jit(solution)/shard_map/ppermute | solution.py:104
  182.4 3.8 %collective-permute-start.9 = (bf16[24,4096]{1,0:T(8,128)(2,1)S(1)}, bf16[24,4096]{1,0:T(8,128)(2,1)S(1)}, u32[]{:S(2)}, u32[]{:S(2)}) collective-permute-start(bf16[24,4096]{1,0:T(8,128)(2,1)S(1)} %get-tuple-element.19), channel_id=1, source_target_pairs={{0,2},{2,4},{4,6},{6,8},{8,10},{10,12},{12,14},{14,0},{1,3},{3,5},... | collective-permute-start | bytes 589832 | tf_op jit(solution)/shard_map/ppermute | solution.py:104
  186.3 1.6 collective-permute-done.13
  187.9 2.7 %collective-permute-done.14 = bf16[24,4096]{1,0:T(8,128)(2,1)S(1)} collective-permute-done((bf16[24,4096]{1,0:T(8,128)(2,1)S(1)}, bf16[24,4096]{1,0:T(8,128)(2,1)S(1)}, u32[]{:S(2)}, u32[]{:S(2)}) %collective-permute-start.14) | collective-permute-done | bytes 196640 | tf_op jit(solution)/shard_map/ppermute | solution.py:104
  190.6 1.0 collective-permute-done.9
  191.6 1.8 fusion.20
  193.4 0.3 reshape.103
  193.7 19.9 %all_to_all.16 = bf16[64,12,128]{2,1,0:T(8,128)(2,1)S(1)} all-to-all(bf16[64,12,128]{2,1,0:T(8,128)(2,1)S(1)} %reshape.103), channel_id=1, replica_groups=mesh['expert'=64,'z'=8,'c'=2] {'expert'}, dimensions={0} | all-to-all | bytes 393216 | tf_op jit(solution)/shard_map/all_to_all | solution.py:226
  213.6 1.1 multiply_subtract_fusion
  (27 shorter events, 0.8 us)
Async XLA Ops:
  0.6 25.4 %copy-start = (bf16[16,8,384]{2,1,0:T(8,128)(2,1)S(1)}, bf16[16,8,384]{2,1,0:T(8,128)(2,1)}, u32[]{:S(2)}) copy-start(bf16[16,8,384]{2,1,0:T(8,128)(2,1)} %param.8) | copy-start | bytes 294916
  2.7 30.4 %all-to-all-start = ((bf16[64,12,128]{2,1,0:T(8,128)(2,1)}), bf16[64,12,128]{2,1,0:T(8,128)(2,1)S(1)}, u32[]{:S(2)}, u32[]{:S(2)}) async-start(bf16[64,12,128]{2,1,0:T(8,128)(2,1)} %reshape.99), calls=%async_computation | async-start | bytes 524288 | tf_op jit(solution)/shard_map/all_to_all | solution.py:168
  75.8 36.8 %collective-permute-start = (bf16[64,96,128]{2,1,0:T(8,128)(2,1)S(1)}, bf16[64,96,128]{2,1,0:T(8,128)(2,1)S(1)}, u32[]{:S(2)}, u32[]{:S(2)}) collective-permute-start(bf16[64,96,128]{2,1,0:T(8,128)(2,1)S(1)} %all_to_all.15), channel_id=1, source_target_pairs={{0,1},{1,0},{2,3},{3,2},{4,5},{5,4},{6,7},{7,6},{8,9},{9,8},{10,11... | collective-permute-start | bytes 4718600 | tf_op jit(solution)/shard_map/ppermute | solution.py:206
  78.6 26.2 %collective-permute-start.1 = (bf16[24,4096]{1,0:T(8,128)(2,1)}, bf16[24,4096]{1,0:T(8,128)(2,1)S(1)}, u32[]{:S(2)}, u32[]{:S(2)}) collective-permute-start(bf16[24,4096]{1,0:T(8,128)(2,1)} %reshape.102.refs_0_), channel_id=1, source_target_pairs={{0,14},{2,0},{4,2},{6,4},{8,6},{10,8},{12,10},{14,12},{1,15},{3,1}... | collective-permute-start | bytes 589832 | tf_op jit(solution)/shard_map/ppermute | solution.py:104
  96.1 13.3 %collective-permute-start.2 = (bf16[24,4096]{1,0:T(8,128)(2,1)}, bf16[24,4096]{1,0:T(8,128)(2,1)S(1)}, u32[]{:S(2)}, u32[]{:S(2)}) collective-permute-start(bf16[24,4096]{1,0:T(8,128)(2,1)} %reshape.102.refs_0_), channel_id=1, source_target_pairs={{0,2},{2,4},{4,6},{6,8},{8,10},{10,12},{12,14},{14,0},{1,3},{3,5},... | collective-permute-start | bytes 589832 | tf_op jit(solution)/shard_map/ppermute | solution.py:104
  98.1 25.0 %collective-permute-start.3 = (bf16[24,4096]{1,0:T(8,128)(2,1)}, bf16[24,4096]{1,0:T(8,128)(2,1)}, u32[]{:S(2)}, u32[]{:S(2)}) collective-permute-start(bf16[24,4096]{1,0:T(8,128)(2,1)} %reshape.102.refs_0_), channel_id=1, source_target_pairs={{0,12},{2,14},{4,0},{6,2},{8,4},{10,6},{12,8},{14,10},{1,13},{3,15... | collective-permute-start | bytes 589832 | tf_op jit(solution)/shard_map/ppermute | solution.py:104
  101.4 21.7 %collective-permute-start.4 = (bf16[24,4096]{1,0:T(8,128)(2,1)}, bf16[24,4096]{1,0:T(8,128)(2,1)}, u32[]{:S(2)}, u32[]{:S(2)}) collective-permute-start(bf16[24,4096]{1,0:T(8,128)(2,1)} %reshape.102.refs_0_), channel_id=1, source_target_pairs={{0,4},{2,6},{4,8},{6,10},{8,12},{10,14},{12,0},{14,2},{1,5},{3,7},... | collective-permute-start | bytes 589832 | tf_op jit(solution)/shard_map/ppermute | solution.py:104
  104.8 16.2 %copy-start.5 = (bf16[24,4096]{1,0:T(8,128)(2,1)}, bf16[24,4096]{1,0:T(8,128)(2,1)S(1)}, u32[]{:S(2)}) copy-start(bf16[24,4096]{1,0:T(8,128)(2,1)S(1)} %collective-permute-done.1.refs_1_) | copy-start | bytes 589828
  104.9 20.0 %collective-permute-start.5 = (bf16[24,4096]{1,0:T(8,128)(2,1)}, bf16[24,4096]{1,0:T(8,128)(2,1)}, u32[]{:S(2)}, u32[]{:S(2)}) collective-permute-start(bf16[24,4096]{1,0:T(8,128)(2,1)} %reshape.102.refs_0_), channel_id=1, source_target_pairs={{0,10},{2,12},{4,14},{6,0},{8,2},{10,4},{12,6},{14,8},{1,11},{3,13... | collective-permute-start | bytes 589832 | tf_op jit(solution)/shard_map/ppermute | solution.py:104
  109.5 3.1 %copy-start.6 = (bf16[24,4096]{1,0:T(8,128)(2,1)}, bf16[24,4096]{1,0:T(8,128)(2,1)S(1)}, u32[]{:S(2)}) copy-start(bf16[24,4096]{1,0:T(8,128)(2,1)S(1)} %collective-permute-done.2.refs_2_) | copy-start | bytes 589828
  109.5 19.3 %collective-permute-start.6 = (bf16[24,4096]{1,0:T(8,128)(2,1)}, bf16[24,4096]{1,0:T(8,128)(2,1)}, u32[]{:S(2)}, u32[]{:S(2)}) collective-permute-start(bf16[24,4096]{1,0:T(8,128)(2,1)} %reshape.102.refs_0_), channel_id=1, source_target_pairs={{0,6},{2,8},{4,10},{6,12},{8,14},{10,0},{12,2},{14,4},{1,7},{3,9},... | collective-permute-start | bytes 589832 | tf_op jit(solution)/shard_map/ppermute | solution.py:104
  112.6 23.4 %collective-permute-start.7 = (bf16[24,4096]{1,0:T(8,128)(2,1)}, bf16[24,4096]{1,0:T(8,128)(2,1)}, u32[]{:S(2)}, u32[]{:S(2)}) collective-permute-start(bf16[24,4096]{1,0:T(8,128)(2,1)} %reshape.102.refs_0_), channel_id=1, source_target_pairs={{0,8},{2,10},{4,12},{6,14},{8,0},{10,2},{12,4},{14,6},{1,9},{3,11}... | collective-permute-start | bytes 589832 | tf_op jit(solution)/shard_map/ppermute | solution.py:104
  146.8 15.3 %collective-permute-start.10 = (bf16[24,4096]{1,0:T(8,128)(2,1)S(1)}, bf16[24,4096]{1,0:T(8,128)(2,1)S(1)}, u32[]{:S(2)}, u32[]{:S(2)}) collective-permute-start(bf16[24,4096]{1,0:T(8,128)(2,1)S(1)} %get-tuple-element.22), channel_id=1, source_target_pairs={{0,12},{2,14},{4,0},{6,2},{8,4},{10,6},{12,8},{14,10},{1,13},{3,15... | collective-permute-start | bytes 589832 | tf_op jit(solution)/shard_map/ppermute | solution.py:104
  153.9 14.8 %collective-permute-start.12 = (bf16[24,4096]{1,0:T(8,128)(2,1)S(1)}, bf16[24,4096]{1,0:T(8,128)(2,1)S(1)}, u32[]{:S(2)}, u32[]{:S(2)}) collective-permute-start(bf16[24,4096]{1,0:T(8,128)(2,1)S(1)} %get-tuple-element.21), channel_id=1, source_target_pairs={{0,4},{1,13},{2,6},{3,15},{4,8},{5,1},{6,10},{7,3},{8,12},{9,5},{1... | collective-permute-start | bytes 589832 | tf_op jit(solution)/shard_map/ppermute | solution.py:112
  155.8 15.0 %collective-permute-start.8 = (bf16[24,4096]{1,0:T(8,128)(2,1)S(1)}, bf16[24,4096]{1,0:T(8,128)(2,1)S(1)}, u32[]{:S(2)}, u32[]{:S(2)}) collective-permute-start(bf16[24,4096]{1,0:T(8,128)(2,1)S(1)} %get-tuple-element.20), channel_id=1, source_target_pairs={{0,4},{2,6},{4,8},{6,10},{8,12},{10,14},{12,0},{14,2},{1,5},{3,7},... | collective-permute-start | bytes 589832 | tf_op jit(solution)/shard_map/ppermute | solution.py:104
  172.2 41.4 %copy-start.1 = (f32[32,1536]{1,0:T(8,128)S(1)}, f32[32,1536]{1,0:T(8,128)}, u32[]{:S(2)}) copy-start(f32[32,1536]{1,0:T(8,128)} %param.11) | copy-start | bytes 589828
  172.3 41.4 %copy-start.2 = (s32[64]{0:T(128)S(1)}, s32[64]{0:T(128)}, u32[]{:S(2)}) copy-start(s32[64]{0:T(128)} %param.10) | copy-start | bytes 772
  172.3 41.3 %copy-start.3 = (f32[32,1536]{1,0:T(8,128)S(1)}, f32[32,1536]{1,0:T(8,128)}, u32[]{:S(2)}) copy-start(f32[32,1536]{1,0:T(8,128)} %param.12) | copy-start | bytes 589828
  172.3 41.3 %copy-start.4 = (f32[32,1536]{1,0:T(8,128)S(1)}, f32[32,1536]{1,0:T(8,128)}, u32[]{:S(2)}) copy-start(f32[32,1536]{1,0:T(8,128)} %param.13) | copy-start | bytes 589828
  172.3 14.0 %collective-permute-start.11 = (bf16[24,4096]{1,0:T(8,128)(2,1)S(1)}, bf16[24,4096]{1,0:T(8,128)(2,1)S(1)}, u32[]{:S(2)}, u32[]{:S(2)}) collective-permute-start(bf16[24,4096]{1,0:T(8,128)(2,1)S(1)} %get-tuple-element.23), channel_id=1, source_target_pairs={{0,14},{2,0},{4,2},{6,4},{8,6},{10,8},{12,10},{14,12},{1,15},{3,1}... | collective-permute-start | bytes 589832 | tf_op jit(solution)/shard_map/ppermute | solution.py:104
  174.5 13.4 %collective-permute-start.13 = (bf16[24,4096]{1,0:T(8,128)(2,1)S(1)}, bf16[24,4096]{1,0:T(8,128)(2,1)S(1)}, u32[]{:S(2)}, u32[]{:S(2)}) collective-permute-start(bf16[24,4096]{1,0:T(8,128)(2,1)S(1)} %get-tuple-element.17), channel_id=1, source_target_pairs={{0,4},{2,6},{4,8},{6,10},{8,12},{10,14},{12,0},{14,2},{1,5},{3,7},... | collective-permute-start | bytes 589832 | tf_op jit(solution)/shard_map/ppermute | solution.py:104
  179.7 10.9 %collective-permute-start.14 = (bf16[24,4096]{1,0:T(8,128)(2,1)S(1)}, bf16[24,4096]{1,0:T(8,128)(2,1)S(1)}, u32[]{:S(2)}, u32[]{:S(2)}) collective-permute-start(bf16[24,4096]{1,0:T(8,128)(2,1)S(1)} %get-tuple-element.18), channel_id=1, source_target_pairs={{0,12},{2,14},{4,0},{6,2},{8,4},{10,6},{12,8},{14,10},{1,13},{3,15... | collective-permute-start | bytes 589832 | tf_op jit(solution)/shard_map/ppermute | solution.py:104
  182.4 9.2 %collective-permute-start.9 = (bf16[24,4096]{1,0:T(8,128)(2,1)S(1)}, bf16[24,4096]{1,0:T(8,128)(2,1)S(1)}, u32[]{:S(2)}, u32[]{:S(2)}) collective-permute-start(bf16[24,4096]{1,0:T(8,128)(2,1)S(1)} %get-tuple-element.19), channel_id=1, source_target_pairs={{0,2},{2,4},{4,6},{6,8},{8,10},{10,12},{12,14},{14,0},{1,3},{3,5},... | collective-permute-start | bytes 589832 | tf_op jit(solution)/shard_map/ppermute | solution.py:104

commit v3 on v2

--- a/solution.py
+++ b/solution.py
@@ -11,6 +11,7 @@
 MOST = 5
 LANES = 128
 CORES = 2
+FAR = 3
 
 
 beta_first = 0.9
@@ -33,17 +34,35 @@
     return (master - learning_rate * update, new_first, new_second)
 
 
-def offset_of(block):
-    return jnp.where(block % 2 == 1, (block + 1) // 2, -(block // 2))
-
-
-def grads_kernel(planes, piece_rows, place, x_own, x_other, *refs):
+def offset_of(block, planes):
+    return jnp.where(block % 2 == 1, (planes - 1 - block) // 2, -((planes - block) // 2))
+
+
+def store_grads(outs, parts, rows_refs, piece_rows, width):
+    tile = 512
+    units = len(outs) * piece_rows
+    for start in range(0, width, tile):
+        cols = slice(start, start + tile)
+        total = jnp.dot(parts[0], rows_refs[0][:, cols], preferred_element_type=jnp.float32)
+        total += jnp.dot(parts[1], rows_refs[1][:, cols], preferred_element_type=jnp.float32)
+        total = total.reshape(2, units, tile)
+        for at, out in enumerate(outs):
+            rows = slice(at * piece_rows, (at + 1) * piece_rows)
+            out[:, start : start + tile] = total[0, rows].astype(jnp.bfloat16)
+            out[:, width + start : width + start + tile] = total[1, rows].astype(jnp.bfloat16)
+
+
+def far_kernel(planes, piece_rows, place, x_own, x_other, *refs):
     f32, bf16 = jnp.float32, jnp.bfloat16
-    pieces, out, weights = refs[:planes], refs[planes], refs[planes + 1]
-    units, width = weights.shape[0], weights.shape[1] // 2
+    pieces, rest = refs[:planes], refs[planes:]
+    outs, d_refs, weights = rest[:FAR], rest[FAR : FAR + CORES], rest[FAR + CORES]
+    units, width = weights.shape[0] // 2, weights.shape[1]
+    for at, piece in enumerate(pieces):
+        lines = slice(at * piece_rows, (at + 1) * piece_rows)
+        weights[lines, :] = piece[:, :width]
+        lines = slice(units + at * piece_rows, units + (at + 1) * piece_rows)
+        weights[lines, :] = piece[:, width:]
     hidden = units * CORES
-    for at, piece in enumerate(pieces):
-        weights[at * piece_rows : (at + 1) * piece_rows, :] = piece[...]
     rows = x_own.shape[0]
     sources = rows // (MOST + 1)
     across = (((1,), (1,)), ((), ()))
@@ -56,14 +75,15 @@
 
     unit = iota((units, hidden), 0)
     block = unit // piece_rows
-    plane = place[0] + offset_of(block) + planes
+    plane = place[0] + offset_of(block, planes) + planes
     plane = jnp.where(plane >= planes, plane - planes, plane)
     plane = jnp.where(plane >= planes, plane - planes, plane)
     column = (plane * CORES + place[1]) * piece_rows + unit - block * piece_rows
     choose = hot(iota((units, hidden), 1) == column)
     last = hot(iota((sources, rows), 1) == iota((sources, rows), 0) * (MOST + 1) + MOST)
-    d_gates, d_ups = [], []
-    for x_ref in (x_own, x_other):
+    far_units = FAR * piece_rows
+    far_parts = []
+    for x_ref, d_ref in zip((x_own, x_other), d_refs):
         packed = jnp.dot(last, x_ref[:, : MOST * hidden], preferred_element_type=f32).astype(bf16)
         dh = jnp.zeros((units, rows), f32)
         for at in range(MOST):
@@ -71,77 +91,63 @@
             mine = lax.dot_general(choose, mine, across, preferred_element_type=f32).astype(bf16)
             spread = hot(iota((sources, rows), 1) == iota((sources, rows), 0) * (MOST + 1) + at)
             dh += jnp.dot(mine, spread, preferred_element_type=f32)
-        values = x_ref[...]
-        gate = lax.dot_general(weights[:, :width], values, across, preferred_element_type=f32)
-        up = lax.dot_general(weights[:, width:], values, across, preferred_element_type=f32)
+        both = lax.dot_general(weights[...], x_ref[...], across, preferred_element_type=f32)
+        gate, up = both[:units], both[units:]
         sig = jax.nn.sigmoid(gate)
-        d_gates.append((dh * up * (sig * (1.0 + gate * (1.0 - sig)))).astype(bf16))
-        d_ups.append((dh * (gate * sig)).astype(bf16))
-    tile = 512
-    for half, parts in enumerate((d_gates, d_ups)):
-        for start in range(0, width, tile):
-            cols = slice(start, start + tile)
-            total = jnp.dot(parts[0], x_own[:, cols], preferred_element_type=f32)
-            total += jnp.dot(parts[1], x_other[:, cols], preferred_element_type=f32)
-            out[:, half * width + start : half * width + start + tile] = total.astype(bf16)
+        d_gate = dh * up * (sig * (1.0 + gate * (1.0 - sig)))
+        d_up = dh * (gate * sig)
+        far_parts.append(
+            jnp.concatenate([d_gate[:far_units], d_up[:far_units]], axis=0).astype(bf16)
+        )
+        d_ref[...] = jnp.concatenate([d_gate[far_units:], d_up[far_units:]], axis=0).astype(bf16)
+    store_grads(outs, far_parts, (x_own, x_other), piece_rows, width)
+
+
+def near_kernel(piece_rows, x_own, x_other, d_own, d_other, *outs):
+    width = x_own.shape[1]
+    store_grads(outs, (d_own[...], d_other[...]), (x_own, x_other), piece_rows, width)
 
 
 def swiglu_grads(planes, piece_rows, place, x_own, x_other, pieces):
-    vmem = pl.BlockSpec(memory_space=pltpu.VMEM)
-    shape = (planes * piece_rows, pieces[0].shape[1])
-    flops = 8 * x_own.shape[0] * shape[0] * shape[1]
-    return pl.pallas_call(
-        functools.partial(grads_kernel, planes, piece_rows),
-        out_shape=jax.ShapeDtypeStruct(shape, jnp.bfloat16),
-        in_specs=[pl.BlockSpec(memory_space=pltpu.SMEM)] + [vmem] * (2 + planes),
-        out_specs=vmem,
-        scratch_shapes=[pltpu.VMEM(shape, jnp.bfloat16)],
-        cost_estimate=pl.CostEstimate(flops=flops, bytes_accessed=8 << 20, transcendentals=0),
+    bf16 = jnp.bfloat16
+    vmem, smem = pl.BlockSpec(memory_space=pltpu.VMEM), pl.BlockSpec(memory_space=pltpu.SMEM)
+    rows, width = x_own.shape
+    units = planes * piece_rows
+    near = planes - FAR
+    block = jax.ShapeDtypeStruct((piece_rows, 2 * width), bf16)
+    d_block = jax.ShapeDtypeStruct((2 * near * piece_rows, rows), bf16)
+    dot_flops = 2 * CORES * rows * 2 * units * width
+    *far_blocks, d_own, d_other = pl.pallas_call(
+        functools.partial(far_kernel, planes, piece_rows),
+        out_shape=[block] * FAR + [d_block] * CORES,
+        in_specs=[smem] + [vmem] * (2 + planes),
+        out_specs=[vmem] * (FAR + CORES),
+        scratch_shapes=[pltpu.VMEM((2 * units, width), bf16)],
+        cost_estimate=pl.CostEstimate(
+            flops=dot_flops * (planes + FAR) // planes, bytes_accessed=6 << 20, transcendentals=0
+        ),
     )(place, x_own, x_other, *pieces)
+    near_blocks = pl.pallas_call(
+        functools.partial(near_kernel, piece_rows),
+        out_shape=[block] * near,
+        in_specs=[vmem] * 4,
+        out_specs=[vmem] * near,
+        cost_estimate=pl.CostEstimate(
+            flops=dot_flops * near // planes, bytes_accessed=4 << 20, transcendentals=0
+        ),
+    )(x_own, x_other, d_own, d_other)
+    return far_blocks, near_blocks
 
 
 def shift(value, planes, by):
     return lax.ppermute(value, "z", [(i, (i - by) % planes) for i in range(planes)])
 
 
-def shift_by_core(value, planes, by):
-    pairs = []
-    for i in range(planes):
-        pairs.append((i * CORES, (i - by) % planes * CORES))
-        pairs.append((i * CORES + 1, (i + by) % planes * CORES + 1))
-    return lax.ppermute(value, ("z", "c"), pairs)
-
-
 def gather_planes(piece, planes):
-    pieces = [piece]
-    for by in range(1, planes // 2):
+    pieces = [shift(piece, planes, planes // 2)]
+    for by in range(planes // 2 - 1, 0, -1):
         pieces += [shift(piece, planes, by), shift(piece, planes, -by)]
-    return pieces + [shift(piece, planes, planes // 2)]
-
-
-def scatter_planes(blocks, planes, core):
-    f32 = jnp.float32
-    own, up1, down1, up2, down2, up3, down3, far = blocks
-    more_up1, more_down1 = shift(up3, planes, -2), shift(down3, planes, 2)
-    more_far = shift_by_core(far, planes, -2).astype(f32)
-    first = core == 0
-
-    def add(value, more):
-        return (value.astype(f32) + more).astype(value.dtype)
-
-    up1, down1 = add(up1, more_up1.astype(f32)), add(down1, more_down1.astype(f32))
-    up2 = add(up2, jnp.where(first, more_far, 0.0))
-    down2 = add(down2, jnp.where(first, 0.0, more_far))
-    parts = [
-        shift(up1, planes, -1),
-        shift(down1, planes, 1),
-        shift(up2, planes, -2),
-        shift(down2, planes, 2),
-    ]
-    total = own.astype(f32)
-    for part in parts:
-        total = total + part.astype(f32)
-    return total
+    return pieces + [piece]
 
 
 def local(tokens, cotangent, expert_ids, placement, master, first_moment, second_moment):
@@ -210,7 +216,7 @@
 
     group = MOST + 1
     place = jnp.stack([lax.axis_index("z"), core])
-    grad_block = swiglu_grads(
+    far_blocks, near_blocks = swiglu_grads(
         planes,
         piece_rows,
         place,
@@ -218,8 +224,13 @@
         other.reshape(slots * group, width),
         pieces,
     )
-    blocks = [grad_block[k * piece_rows : (k + 1) * piece_rows] for k in range(planes)]
-    summed = scatter_planes(blocks, planes, core)
+    parts = [shift(far_blocks[0], planes, planes // 2)]
+    parts += [shift(far_blocks[1], planes, -3), shift(far_blocks[2], planes, 3)]
+    parts += [shift(near_blocks[0], planes, -2), shift(near_blocks[1], planes, 2)]
+    parts += [shift(near_blocks[2], planes, -1), shift(near_blocks[3], planes, 1)]
+    summed = near_blocks[4].astype(f32)
+    for part in parts:
+        summed = summed + part.astype(f32)
     replica_grad = summed[None]
 
     outgoing = summed.astype(bf16).reshape(slots, shard_width // LANES, LANES)

time: 216 us -> 218 us (level)
  starting transfers between devices: 87.8 us -> 84.8 us
  Pallas kernels: 9.69 us -> 12 us
    ppermute x13 -> x14, waiting for transfers between devices: 20.5 us -> 30.9 us  [shift(): lax.ppermute(value, 'z', [(i, (i - by) % planes) for i in range(planes)])]
    ppermute x1 -> x0, waiting for transfers between devices: 6.6 us -> none  [shift_by_core(): return lax.ppermute(value, ('z', 'c'), pairs)]
    pallas_call x1 -> x2, Pallas kernels: 9.69 us -> 12 us  [the longest x1 7.97 us: swiglu_grads(): pl.pallas_call(functools.partial(far_kernel, planes, piece_rows), out_sha...]
    ppermute x13 -> x14, starting transfers between devices: 66.7 us -> 65.6 us  [shift(): lax.ppermute(value, 'z', [(i, (i - by) % planes) for i in range(planes)])]
  transfers between devices with their start and end apart: 16 -> 16, of which waited for: 10 -> 5; matrix products, arithmetic and copies ran while one was open for 6% -> 7% of each run, Pallas kernels for 0% -> 0%
where the time goes in v3:
time: 218 us; the launch traced here: 217 us
  starting transfers between devices  84.8 us (39%)
  blocking collectives  64.6 us (30%)
  waiting for transfers between devices  34.9 us (16%)
  Pallas kernels  12 us (6%)
  local copies, waits for them, and re-layouts  8.8 us (4%)
  other arithmetic  7.2 us (3%)
  matrix products  4.16 us (2%)
    ppermute x14, starting transfers between devices, shift(): lax.ppermute(value, 'z', [(i, (i - by) % planes) for i in range(planes)])  65.6 us
    all_to_all x1, blocking collectives, local(): lax.all_to_all(send, 'expert', split_axis=0, concat_axis=0, tiled=True)  44.8 us
    ppermute x14, waiting for transfers between devices, shift(): lax.ppermute(value, 'z', [(i, (i - by) % planes) for i in range(planes)])  30.9 us
    all_to_all x1, blocking collectives, local(): lax.all_to_all(outgoing, 'expert', split_axis=0, concat_axis=0, tiled=True)  19.8 us
    all_to_all x1, starting transfers between devices, local(): lax.all_to_all(send_weight, 'expert', split_axis=0, concat_axis=0, tiled=...  17.2 us
    pallas_call x1, Pallas kernels, swiglu_grads(): pl.pallas_call(functools.partial(far_kernel, planes, piece_rows), out_sha...  7.97 us
  transfers between devices with their start and end apart: 16, of which 5 were waited for; matrix products, arithmetic and copies ran while one was open for 7% of the time, Pallas kernels for 0%

profile of v3, /device:TPU:2, one launch (start us, length us, event | category | flops | bytes accessed | tf_op | source)
XLA Modules:
  0.0 217.5 jit_solution(4815117300521400024)
XLA Ops:
  0.6 1.2 convolution_convert_fusion.1
  1.9 0.9 reshape.99
  2.7 17.2 %all-to-all-start = ((bf16[64,12,128]{2,1,0:T(8,128)(2,1)}), bf16[64,12,128]{2,1,0:T(8,128)(2,1)S(1)}, u32[]{:S(2)}, u32[]{:S(2)}) async-start(bf16[64,12,128]{2,1,0:T(8,128)(2,1)} %reshape.99), calls=%async_computation | async-start | bytes 524288 | tf_op jit(solution)/shard_map/all_to_all | solution.py:174
  20.0 0.9 convert_reduce_fusion.1
  20.9 0.8 convert_reduce_fusion.2
  21.6 0.8 copy.13
  22.4 0.1 eq.105
  22.5 0.2 convert_reduce_fusion
  22.7 0.1 and_select_fusion.1
  22.8 0.8 select_reduce_fusion.1
  23.6 0.1 select_reduce_fusion
  23.7 1.6 convolution_convert_fusion
  25.4 0.2 convolution_convert_fusion.2
  25.6 0.2 reshape.98
  25.8 1.5 reshape.96
  27.3 0.1 pad.4.clone
  27.3 1.7 maximum_maximum_fusion
  29.0 4.1 %all-to-all-done = bf16[64,12,128]{2,1,0:T(8,128)(2,1)S(1)} async-done(((bf16[64,12,128]{2,1,0:T(8,128)(2,1)}), bf16[64,12,128]{2,1,0:T(8,128)(2,1)S(1)}, u32[]{:S(2)}, u32[]{:S(2)}) %all-to-all-start) | async-done | bytes 196640 | tf_op jit(solution)/shard_map/all_to_all | solution.py:174
  33.1 44.8 %all_to_all.15 = bf16[64,96,128]{2,1,0:T(8,128)(2,1)S(1)} all-to-all(bf16[64,96,128]{2,1,0:T(8,128)(2,1)S(1)} %maximum_maximum_fusion), channel_id=1, replica_groups=mesh['expert'=64,'z'=8,'c'=2] {'expert'}, dimensions={0} | all-to-all | bytes 3145728 | tf_op jit(solution)/shard_map/all_to_all | solution.py:211
  77.9 1.9 collective-permute-start
  79.8 0.9 reshape.102.refs_7_
  80.7 14.8 %collective-permute-start.1 = (bf16[24,4096]{1,0:T(8,128)(2,1)}, bf16[24,4096]{1,0:T(8,128)(2,1)S(1)}, u32[]{:S(2)}, u32[]{:S(2)}) collective-permute-start(bf16[24,4096]{1,0:T(8,128)(2,1)} %reshape.102.refs_7_), channel_id=1, source_target_pairs={{0,8},{2,10},{4,12},{6,14},{8,0},{10,2},{12,4},{14,6},{1,9},{3,11}... | collective-permute-start | bytes 589832 | tf_op jit(solution)/shard_map/ppermute | solution.py:143
  95.5 2.8 %collective-permute-start.2 = (bf16[24,4096]{1,0:T(8,128)(2,1)}, bf16[24,4096]{1,0:T(8,128)(2,1)S(1)}, u32[]{:S(2)}, u32[]{:S(2)}) collective-permute-start(bf16[24,4096]{1,0:T(8,128)(2,1)} %reshape.102.refs_7_), channel_id=1, source_target_pairs={{0,10},{2,12},{4,14},{6,0},{8,2},{10,4},{12,6},{14,8},{1,11},{3,13... | collective-permute-start | bytes 589832 | tf_op jit(solution)/shard_map/ppermute | solution.py:143
  98.4 7.0 %collective-permute-start.3 = (bf16[24,4096]{1,0:T(8,128)(2,1)}, bf16[24,4096]{1,0:T(8,128)(2,1)}, u32[]{:S(2)}, u32[]{:S(2)}) collective-permute-start(bf16[24,4096]{1,0:T(8,128)(2,1)} %reshape.102.refs_7_), channel_id=1, source_target_pairs={{0,6},{2,8},{4,10},{6,12},{8,14},{10,0},{12,2},{14,4},{1,7},{3,9},... | collective-permute-start | bytes 589832 | tf_op jit(solution)/shard_map/ppermute | solution.py:143
  105.4 4.6 %collective-permute-start.4 = (bf16[24,4096]{1,0:T(8,128)(2,1)}, bf16[24,4096]{1,0:T(8,128)(2,1)}, u32[]{:S(2)}, u32[]{:S(2)}) collective-permute-start(bf16[24,4096]{1,0:T(8,128)(2,1)} %reshape.102.refs_7_), channel_id=1, source_target_pairs={{0,12},{2,14},{4,0},{6,2},{8,4},{10,6},{12,8},{14,10},{1,13},{3,15... | collective-permute-start | bytes 589832 | tf_op jit(solution)/shard_map/ppermute | solution.py:143
  110.0 2.5 %collective-permute-start.5 = (bf16[24,4096]{1,0:T(8,128)(2,1)}, bf16[24,4096]{1,0:T(8,128)(2,1)}, u32[]{:S(2)}, u32[]{:S(2)}) collective-permute-start(bf16[24,4096]{1,0:T(8,128)(2,1)} %reshape.102.refs_7_), channel_id=1, source_target_pairs={{0,4},{2,6},{4,8},{6,10},{8,12},{10,14},{12,0},{14,2},{1,5},{3,7},... | collective-permute-start | bytes 589832 | tf_op jit(solution)/shard_map/ppermute | solution.py:143
  112.5 10.0 %collective-permute-done.2.refs_1_ = bf16[24,4096]{1,0:T(8,128)(2,1)S(1)} collective-permute-done((bf16[24,4096]{1,0:T(8,128)(2,1)}, bf16[24,4096]{1,0:T(8,128)(2,1)S(1)}, u32[]{:S(2)}, u32[]{:S(2)}) %collective-permute-start.2) | collective-permute-done | bytes 196640 | tf_op jit(solution)/shard_map/ppermute | solution.py:143
  122.4 1.9 collective-permute-start.6
  124.4 3.9 %collective-permute-start.7 = (bf16[24,4096]{1,0:T(8,128)(2,1)}, bf16[24,4096]{1,0:T(8,128)(2,1)}, u32[]{:S(2)}, u32[]{:S(2)}) collective-permute-start(bf16[24,4096]{1,0:T(8,128)(2,1)} %reshape.102.refs_7_), channel_id=1, source_target_pairs={{0,2},{2,4},{4,6},{6,8},{8,10},{10,12},{12,14},{14,0},{1,3},{3,5},... | collective-permute-start | bytes 589832 | tf_op jit(solution)/shard_map/ppermute | solution.py:143
  128.3 0.6 pad_add_fusion.place
  128.9 2.1 reshape.100.x_own
  131.0 2.1 reshape.101.x_other
  133.1 1.4 collective-permute-done.7.refs_6_
  134.6 8.0 %shard_map.102 = (bf16[24,4096]{1,0:T(8,128)(2,1)}, bf16[24,4096]{1,0:T(8,128)(2,1)}, bf16[24,4096]{1,0:T(8,128)(2,1)}, bf16[240,384]{1,0:T(8,128)(2,1)}, bf16[240,384]{1,0:T(8,128)(2,1)}) custom-call(s32[2]{0:T(128)} %pad_add_fusion.place, bf16[384,2048]{1,0:T(8,128)(2,1)} %reshape.100.x_own, bf16[384,2048]{1,0:T(8,128)(2,1)} %reshape.101.x_other, ...), custom_call_target="tpu_custom_call" | custom-call | flops 1660944384 | bytes 6291456 | tf_op jit(solution)/shard_map/pallas_call | solution.py:120
  142.5 4.1 %shard_map.103 = (bf16[24,4096]{1,0:T(8,128)(2,1)}, bf16[24,4096]{1,0:T(8,128)(2,1)}, bf16[24,4096]{1,0:T(8,128)(2,1)}, bf16[24,4096]{1,0:T(8,128)(2,1)}, bf16[24,4096]{1,0:T(8,128)(2,1)}) custom-call(bf16[384,2048]{1,0:T(8,128)(2,1)} %reshape.100.x_own, bf16[384,2048]{1,0:T(8,128)(2,1)} %reshape.101.x_other, bf16[240,384]{1,0:T(8,128)(2,1)} %get-tuple-element.20.d_own, ...), custom_call_target="tpu_custom_call" | custom-call | flops 754974720 | bytes 4194304 | tf_op jit(solution)/shard_map/pallas_call | solution.py:130
  146.6 3.9 %collective-permute-start.14 = (bf16[24,4096]{1,0:T(8,128)(2,1)}, bf16[24,4096]{1,0:T(8,128)(2,1)S(1)}, u32[]{:S(2)}, u32[]{:S(2)}) collective-permute-start(bf16[24,4096]{1,0:T(8,128)(2,1)} %get-tuple-element.29), channel_id=1, source_target_pairs={{0,14},{2,0},{4,2},{6,4},{8,6},{10,8},{12,10},{14,12},{1,15},{3,1}... | collective-permute-start | bytes 589832 | tf_op jit(solution)/shard_map/ppermute | solution.py:143
  150.5 1.9 collective-permute-start.13
  152.5 4.5 %collective-permute-start.12 = (bf16[24,4096]{1,0:T(8,128)(2,1)}, bf16[24,4096]{1,0:T(8,128)(2,1)S(1)}, u32[]{:S(2)}, u32[]{:S(2)}) collective-permute-start(bf16[24,4096]{1,0:T(8,128)(2,1)} %get-tuple-element.27), channel_id=1, source_target_pairs={{0,12},{2,14},{4,0},{6,2},{8,4},{10,6},{12,8},{14,10},{1,13},{3,15... | collective-permute-start | bytes 589832 | tf_op jit(solution)/shard_map/ppermute | solution.py:143
  156.9 2.3 %collective-permute-start.11 = (bf16[24,4096]{1,0:T(8,128)(2,1)}, bf16[24,4096]{1,0:T(8,128)(2,1)S(1)}, u32[]{:S(2)}, u32[]{:S(2)}) collective-permute-start(bf16[24,4096]{1,0:T(8,128)(2,1)} %get-tuple-element.26), channel_id=1, source_target_pairs={{0,4},{2,6},{4,8},{6,10},{8,12},{10,14},{12,0},{14,2},{1,5},{3,7},... | collective-permute-start | bytes 589832 | tf_op jit(solution)/shard_map/ppermute | solution.py:143
  159.2 6.5 %collective-permute-start.10 = (bf16[24,4096]{1,0:T(8,128)(2,1)S(1)}, bf16[24,4096]{1,0:T(8,128)(2,1)S(1)}, u32[]{:S(2)}, u32[]{:S(2)}) collective-permute-start(bf16[24,4096]{1,0:T(8,128)(2,1)S(1)} %copy-done.9), channel_id=1, source_target_pairs={{0,10},{2,12},{4,14},{6,0},{8,2},{10,4},{12,6},{14,8},{1,11},{3,13... | collective-permute-start | bytes 589832 | tf_op jit(solution)/shard_map/ppermute | solution.py:143
  165.7 3.2 %collective-permute-start.9 = (bf16[24,4096]{1,0:T(8,128)(2,1)S(1)}, bf16[24,4096]{1,0:T(8,128)(2,1)S(1)}, u32[]{:S(2)}, u32[]{:S(2)}) collective-permute-start(bf16[24,4096]{1,0:T(8,128)(2,1)S(1)} %copy-done.8), channel_id=1, source_target_pairs={{0,6},{2,8},{4,10},{6,12},{8,14},{10,0},{12,2},{14,4},{1,7},{3,9},... | collective-permute-start | bytes 589832 | tf_op jit(solution)/shard_map/ppermute | solution.py:143
  168.9 5.9 %collective-permute-start.8 = (bf16[24,4096]{1,0:T(8,128)(2,1)S(1)}, bf16[24,4096]{1,0:T(8,128)(2,1)S(1)}, u32[]{:S(2)}, u32[]{:S(2)}) collective-permute-start(bf16[24,4096]{1,0:T(8,128)(2,1)S(1)} %copy-done.6), channel_id=1, source_target_pairs={{0,8},{2,10},{4,12},{6,14},{8,0},{10,2},{12,4},{14,6},{1,9},{3,11}... | collective-permute-start | bytes 589832 | tf_op jit(solution)/shard_map/ppermute | solution.py:143
  174.9 10.0 %collective-permute-done.10 = bf16[24,4096]{1,0:T(8,128)(2,1)S(1)} collective-permute-done((bf16[24,4096]{1,0:T(8,128)(2,1)S(1)}, bf16[24,4096]{1,0:T(8,128)(2,1)S(1)}, u32[]{:S(2)}, u32[]{:S(2)}) %collective-permute-start.10) | collective-permute-done | bytes 196640 | tf_op jit(solution)/shard_map/ppermute | solution.py:143
  184.9 9.4 %collective-permute-done.8 = bf16[24,4096]{1,0:T(8,128)(2,1)S(1)} collective-permute-done((bf16[24,4096]{1,0:T(8,128)(2,1)S(1)}, bf16[24,4096]{1,0:T(8,128)(2,1)S(1)}, u32[]{:S(2)}, u32[]{:S(2)}) %collective-permute-start.8) | collective-permute-done | bytes 196640 | tf_op jit(solution)/shard_map/ppermute | solution.py:143
  194.3 1.9 fusion.17
  196.3 0.3 reshape.103
  196.5 19.8 %all_to_all.16 = bf16[64,12,128]{2,1,0:T(8,128)(2,1)S(1)} all-to-all(bf16[64,12,128]{2,1,0:T(8,128)(2,1)S(1)} %reshape.103), channel_id=1, replica_groups=mesh['expert'=64,'z'=8,'c'=2] {'expert'}, dimensions={0} | all-to-all | bytes 393216 | tf_op jit(solution)/shard_map/all_to_all | solution.py:237
  216.4 1.1 multiply_subtract_fusion
  (32 shorter events, 0.1 us)
Async XLA Ops:
  0.6 24.8 %copy-start = (bf16[16,8,384]{2,1,0:T(8,128)(2,1)S(1)}, bf16[16,8,384]{2,1,0:T(8,128)(2,1)}, u32[]{:S(2)}) copy-start(bf16[16,8,384]{2,1,0:T(8,128)(2,1)} %param.8) | copy-start | bytes 294916
  2.7 30.4 %all-to-all-start = ((bf16[64,12,128]{2,1,0:T(8,128)(2,1)}), bf16[64,12,128]{2,1,0:T(8,128)(2,1)S(1)}, u32[]{:S(2)}, u32[]{:S(2)}) async-start(bf16[64,12,128]{2,1,0:T(8,128)(2,1)} %reshape.99), calls=%async_computation | async-start | bytes 524288 | tf_op jit(solution)/shard_map/all_to_all | solution.py:174
  77.9 46.5 %collective-permute-start = (bf16[64,96,128]{2,1,0:T(8,128)(2,1)S(1)}, bf16[64,96,128]{2,1,0:T(8,128)(2,1)S(1)}, u32[]{:S(2)}, u32[]{:S(2)}) collective-permute-start(bf16[64,96,128]{2,1,0:T(8,128)(2,1)S(1)} %all_to_all.15), channel_id=1, source_target_pairs={{0,1},{1,0},{2,3},{3,2},{4,5},{5,4},{6,7},{7,6},{8,9},{9,8},{10,11... | collective-permute-start | bytes 4718600 | tf_op jit(solution)/shard_map/ppermute | solution.py:212
  80.7 29.3 %collective-permute-start.1 = (bf16[24,4096]{1,0:T(8,128)(2,1)}, bf16[24,4096]{1,0:T(8,128)(2,1)S(1)}, u32[]{:S(2)}, u32[]{:S(2)}) collective-permute-start(bf16[24,4096]{1,0:T(8,128)(2,1)} %reshape.102.refs_7_), channel_id=1, source_target_pairs={{0,8},{2,10},{4,12},{6,14},{8,0},{10,2},{12,4},{14,6},{1,9},{3,11}... | collective-permute-start | bytes 589832 | tf_op jit(solution)/shard_map/ppermute | solution.py:143
  95.5 26.9 %collective-permute-start.2 = (bf16[24,4096]{1,0:T(8,128)(2,1)}, bf16[24,4096]{1,0:T(8,128)(2,1)S(1)}, u32[]{:S(2)}, u32[]{:S(2)}) collective-permute-start(bf16[24,4096]{1,0:T(8,128)(2,1)} %reshape.102.refs_7_), channel_id=1, source_target_pairs={{0,10},{2,12},{4,14},{6,0},{8,2},{10,4},{12,6},{14,8},{1,11},{3,13... | collective-permute-start | bytes 589832 | tf_op jit(solution)/shard_map/ppermute | solution.py:143
  98.4 34.7 %collective-permute-start.3 = (bf16[24,4096]{1,0:T(8,128)(2,1)}, bf16[24,4096]{1,0:T(8,128)(2,1)}, u32[]{:S(2)}, u32[]{:S(2)}) collective-permute-start(bf16[24,4096]{1,0:T(8,128)(2,1)} %reshape.102.refs_7_), channel_id=1, source_target_pairs={{0,6},{2,8},{4,10},{6,12},{8,14},{10,0},{12,2},{14,4},{1,7},{3,9},... | collective-permute-start | bytes 589832 | tf_op jit(solution)/shard_map/ppermute | solution.py:143
  105.4 27.7 %collective-permute-start.4 = (bf16[24,4096]{1,0:T(8,128)(2,1)}, bf16[24,4096]{1,0:T(8,128)(2,1)}, u32[]{:S(2)}, u32[]{:S(2)}) collective-permute-start(bf16[24,4096]{1,0:T(8,128)(2,1)} %reshape.102.refs_7_), channel_id=1, source_target_pairs={{0,12},{2,14},{4,0},{6,2},{8,4},{10,6},{12,8},{14,10},{1,13},{3,15... | collective-permute-start | bytes 589832 | tf_op jit(solution)/shard_map/ppermute | solution.py:143
  110.0 21.0 %copy-start.5 = (bf16[24,4096]{1,0:T(8,128)(2,1)}, bf16[24,4096]{1,0:T(8,128)(2,1)S(1)}, u32[]{:S(2)}) copy-start(bf16[24,4096]{1,0:T(8,128)(2,1)S(1)} %collective-permute-done.1.refs_0_) | copy-start | bytes 589828
  110.0 23.1 %collective-permute-start.5 = (bf16[24,4096]{1,0:T(8,128)(2,1)}, bf16[24,4096]{1,0:T(8,128)(2,1)}, u32[]{:S(2)}, u32[]{:S(2)}) collective-permute-start(bf16[24,4096]{1,0:T(8,128)(2,1)} %reshape.102.refs_7_), channel_id=1, source_target_pairs={{0,4},{2,6},{4,8},{6,10},{8,12},{10,14},{12,0},{14,2},{1,5},{3,7},... | collective-permute-start | bytes 589832 | tf_op jit(solution)/shard_map/ppermute | solution.py:143
  122.4 1.9 copy-start.7
  122.4 10.7 %collective-permute-start.6 = (bf16[24,4096]{1,0:T(8,128)(2,1)}, bf16[24,4096]{1,0:T(8,128)(2,1)}, u32[]{:S(2)}, u32[]{:S(2)}) collective-permute-start(bf16[24,4096]{1,0:T(8,128)(2,1)} %reshape.102.refs_7_), channel_id=1, source_target_pairs={{0,14},{2,0},{4,2},{6,4},{8,6},{10,8},{12,10},{14,12},{1,15},{3,1}... | collective-permute-start | bytes 589832 | tf_op jit(solution)/shard_map/ppermute | solution.py:143
  124.4 10.2 %collective-permute-start.7 = (bf16[24,4096]{1,0:T(8,128)(2,1)}, bf16[24,4096]{1,0:T(8,128)(2,1)}, u32[]{:S(2)}, u32[]{:S(2)}) collective-permute-start(bf16[24,4096]{1,0:T(8,128)(2,1)} %reshape.102.refs_7_), channel_id=1, source_target_pairs={{0,2},{2,4},{4,6},{6,8},{8,10},{10,12},{12,14},{14,0},{1,3},{3,5},... | collective-permute-start | bytes 589832 | tf_op jit(solution)/shard_map/ppermute | solution.py:143
  142.5 16.7 %copy-start.9 = (bf16[24,4096]{1,0:T(8,128)(2,1)S(1)}, bf16[24,4096]{1,0:T(8,128)(2,1)}, u32[]{:S(2)}) copy-start(bf16[24,4096]{1,0:T(8,128)(2,1)} %get-tuple-element.25) | copy-start | bytes 589828
  142.5 23.2 %copy-start.8 = (bf16[24,4096]{1,0:T(8,128)(2,1)S(1)}, bf16[24,4096]{1,0:T(8,128)(2,1)}, u32[]{:S(2)}) copy-start(bf16[24,4096]{1,0:T(8,128)(2,1)} %get-tuple-element.24) | copy-start | bytes 589828
  142.5 26.4 %copy-start.6 = (bf16[24,4096]{1,0:T(8,128)(2,1)S(1)}, bf16[24,4096]{1,0:T(8,128)(2,1)}, u32[]{:S(2)}) copy-start(bf16[24,4096]{1,0:T(8,128)(2,1)} %get-tuple-element.23) | copy-start | bytes 589828
  146.6 19.1 %collective-permute-start.14 = (bf16[24,4096]{1,0:T(8,128)(2,1)}, bf16[24,4096]{1,0:T(8,128)(2,1)S(1)}, u32[]{:S(2)}, u32[]{:S(2)}) collective-permute-start(bf16[24,4096]{1,0:T(8,128)(2,1)} %get-tuple-element.29), channel_id=1, source_target_pairs={{0,14},{2,0},{4,2},{6,4},{8,6},{10,8},{12,10},{14,12},{1,15},{3,1}... | collective-permute-start | bytes 589832 | tf_op jit(solution)/shard_map/ppermute | solution.py:143
  150.5 18.4 %collective-permute-start.13 = (bf16[24,4096]{1,0:T(8,128)(2,1)}, bf16[24,4096]{1,0:T(8,128)(2,1)S(1)}, u32[]{:S(2)}, u32[]{:S(2)}) collective-permute-start(bf16[24,4096]{1,0:T(8,128)(2,1)} %get-tuple-element.28), channel_id=1, source_target_pairs={{0,2},{2,4},{4,6},{6,8},{8,10},{10,12},{12,14},{14,0},{1,3},{3,5},... | collective-permute-start | bytes 589832 | tf_op jit(solution)/shard_map/ppermute | solution.py:143
  152.5 22.4 %collective-permute-start.12 = (bf16[24,4096]{1,0:T(8,128)(2,1)}, bf16[24,4096]{1,0:T(8,128)(2,1)S(1)}, u32[]{:S(2)}, u32[]{:S(2)}) collective-permute-start(bf16[24,4096]{1,0:T(8,128)(2,1)} %get-tuple-element.27), channel_id=1, source_target_pairs={{0,12},{2,14},{4,0},{6,2},{8,4},{10,6},{12,8},{14,10},{1,13},{3,15... | collective-permute-start | bytes 589832 | tf_op jit(solution)/shard_map/ppermute | solution.py:143
  156.9 17.9 %collective-permute-start.11 = (bf16[24,4096]{1,0:T(8,128)(2,1)}, bf16[24,4096]{1,0:T(8,128)(2,1)S(1)}, u32[]{:S(2)}, u32[]{:S(2)}) collective-permute-start(bf16[24,4096]{1,0:T(8,128)(2,1)} %get-tuple-element.26), channel_id=1, source_target_pairs={{0,4},{2,6},{4,8},{6,10},{8,12},{10,14},{12,0},{14,2},{1,5},{3,7},... | collective-permute-start | bytes 589832 | tf_op jit(solution)/shard_map/ppermute | solution.py:143
  159.2 25.6 %collective-permute-start.10 = (bf16[24,4096]{1,0:T(8,128)(2,1)S(1)}, bf16[24,4096]{1,0:T(8,128)(2,1)S(1)}, u32[]{:S(2)}, u32[]{:S(2)}) collective-permute-start(bf16[24,4096]{1,0:T(8,128)(2,1)S(1)} %copy-done.9), channel_id=1, source_target_pairs={{0,10},{2,12},{4,14},{6,0},{8,2},{10,4},{12,6},{14,8},{1,11},{3,13... | collective-permute-start | bytes 589832 | tf_op jit(solution)/shard_map/ppermute | solution.py:143
  165.7 19.1 %collective-permute-start.9 = (bf16[24,4096]{1,0:T(8,128)(2,1)S(1)}, bf16[24,4096]{1,0:T(8,128)(2,1)S(1)}, u32[]{:S(2)}, u32[]{:S(2)}) collective-permute-start(bf16[24,4096]{1,0:T(8,128)(2,1)S(1)} %copy-done.8), channel_id=1, source_target_pairs={{0,6},{2,8},{4,10},{6,12},{8,14},{10,0},{12,2},{14,4},{1,7},{3,9},... | collective-permute-start | bytes 589832 | tf_op jit(solution)/shard_map/ppermute | solution.py:143
  168.9 25.4 %collective-permute-start.8 = (bf16[24,4096]{1,0:T(8,128)(2,1)S(1)}, bf16[24,4096]{1,0:T(8,128)(2,1)S(1)}, u32[]{:S(2)}, u32[]{:S(2)}) collective-permute-start(bf16[24,4096]{1,0:T(8,128)(2,1)S(1)} %copy-done.6), channel_id=1, source_target_pairs={{0,8},{2,10},{4,12},{6,14},{8,0},{10,2},{12,4},{14,6},{1,9},{3,11}... | collective-permute-start | bytes 589832 | tf_op jit(solution)/shard_map/ppermute | solution.py:143
  194.3 22.1 %copy-start.1 = (f32[32,1536]{1,0:T(8,128)S(1)}, f32[32,1536]{1,0:T(8,128)}, u32[]{:S(2)}) copy-start(f32[32,1536]{1,0:T(8,128)} %param.11) | copy-start | bytes 589828
  194.3 22.1 %copy-start.2 = (s32[64]{0:T(128)S(1)}, s32[64]{0:T(128)}, u32[]{:S(2)}) copy-start(s32[64]{0:T(128)} %param.10) | copy-start | bytes 772
  194.3 22.1 %copy-start.3 = (f32[32,1536]{1,0:T(8,128)S(1)}, f32[32,1536]{1,0:T(8,128)}, u32[]{:S(2)}) copy-start(f32[32,1536]{1,0:T(8,128)} %param.12) | copy-start | bytes 589828
  194.3 22.1 %copy-start.4 = (f32[32,1536]{1,0:T(8,128)S(1)}, f32[32,1536]{1,0:T(8,128)}, u32[]{:S(2)}) copy-start(f32[32,1536]{1,0:T(8,128)} %param.13) | copy-start | bytes 589828
